TPU v7x, 32 devices: a whole 2x2x4 slice. The times are simulated.
32 devices in a mesh: dp: 2 (over x), expert: 8 (over z, y), tensor: 2 (over core).
Axes of the slice: x: 2, y: 2, z: 4, core: 2. Of those that a mesh axis runs over, the one named last changes fastest.
Arguments:
- activations: bfloat16 [4096, 1536], P(('dp', 'expert', 'tensor')), may hold values from -6 to 6
- segments: int32 [16, 256], P(('dp', 'expert')), may hold values from 0 to 3, never falling along the last dimension, each value on 1 to 128 neighbouring positions
- routes: int32 [4096, 8], P(('dp', 'expert', 'tensor')), may hold values from 0 to 15, all different within a row; in each aligned block of 128 rows (0 to 127, 128 to 255, ...) at most 128 rows name the same one
- route_weights: float32 [4096, 8], P(('dp', 'expert', 'tensor')), may hold values from 0.03 to 0.3
- norm_attn_gain: float32 [1536], replicated, may hold values from 0.5 to 1.5
- norm_ffn_gain: float32 [1536], replicated, may hold values from 0.5 to 1.5
- query_weight: bfloat16 [1536, 1536], P(None, 'tensor'), may hold values from -0.15625 to 0.15625
- key_matrix: bfloat16 [1536, 512], P(None, 'tensor'), may hold values from -0.15625 to 0.15625
- value_matrix: bfloat16 [1536, 512], P(None, 'tensor'), may hold values from -0.15625 to 0.15625
- output_projection_weight: bfloat16 [1536, 1536], P('tensor'), may hold values from -0.625 to 0.625
- expert_gate: bfloat16 [16, 1536, 512], P('expert', None, 'tensor'), may hold values from -0.15625 to 0.15625
- expert_up: bfloat16 [16, 1536, 512], P('expert', None, 'tensor'), may hold values from -0.15625 to 0.15625
- expert_down: bfloat16 [16, 512, 1536], P('expert', 'tensor'), may hold values from -0.5 to 0.5
- grad_output: bfloat16 [4096, 1536], P(('dp', 'expert', 'tensor')), may hold values from -6 to 6
Outputs:
- block_out: bfloat16 [4096, 1536], P(('dp', 'expert', 'tensor'))
- grad_input: float32 [4096, 1536], P(('dp', 'expert', 'tensor'))
- grad_norm_attn: float32 [1536], replicated
- grad_norm_ffn: float32 [1536], replicated
- grad_query: float32 [1536, 1536], P(None, 'tensor')
- grad_key: float32 [1536, 512], P(None, 'tensor')
- grad_value: float32 [1536, 512], P(None, 'tensor')
- grad_mixer: float32 [1536, 1536], P('tensor')
- grad_expert_gate: float32 [16, 1536, 512], P('expert', None, 'tensor')
- grad_expert_up: float32 [16, 1536, 512], P('expert', None, 'tensor')
- grad_expert_down: float32 [16, 512, 1536], P('expert', 'tensor')
Inputs may be any that keep to these rules, and one draw needn't show every extreme that they name: `routes`: each row names 8 different experts; in the rows of one device (aligned blocks of 128 rows) no expert is named more than 128 times, and one is named exactly 128 times in some block. `segments`: each sequence's numbers never fall; 4 documents of 1 to 128 positions, one of exactly 128.
All inputs are finite; a program needn't handle non-finite values.
Results may differ from a plain program's by a relative error of at most 0.01.
Values may be sent and summed in bfloat16 or wider, within the bound.
No kernel may reach another device: no remote copies, remote signals or barrier semaphores. Data moves between devices by JAX's collectives and lax.ppermute only.
A program may use at most 320 MiB of HBM per device.

v0:
```python
import jax
import jax.numpy as jnp
from jax import lax
from jax.sharding import PartitionSpec as P

HEAD_DIM = 64


EPS = 1e-05
ATTN_SCALE = 0.015625
THETA = 10000.0
NEG_FILL = -1e30


def norm_forward(values, gain_vector):
    inv_scale = lax.rsqrt(jnp.mean(values * values, axis=-1, keepdims=True) + EPS)
    return (values * inv_scale * gain_vector, inv_scale)


def norm_backward(values, inv_scale, gain_vector, upstream):
    weighted = upstream * gain_vector
    inner = jnp.mean(weighted * values, axis=-1, keepdims=True)
    value_gradient = inv_scale * weighted - values * (inv_scale * inv_scale * inv_scale) * inner
    grad_gain = jnp.sum(upstream * values * inv_scale, axis=0)
    return (value_gradient, grad_gain)


def rope_tables(length, head_size):
    position = jnp.arange(length, dtype=jnp.float32)
    frequency = THETA ** (-jnp.arange(head_size // 2, dtype=jnp.float32) * 2.0 / head_size)
    angle_table = position[:, None] * frequency[None, :]
    return (jnp.cos(angle_table)[:, None, :], jnp.sin(angle_table)[:, None, :])


def apply_rotary(field_in, cosine_lookup, sine_lookup):
    half_size = field_in.shape[-1] // 2
    first_half = field_in[..., :half_size]
    second_half = field_in[..., half_size:]
    return jnp.concatenate(
        [
            first_half * cosine_lookup - second_half * sine_lookup,
            second_half * cosine_lookup + first_half * sine_lookup,
        ],
        axis=-1,
    )


def invert_rotary(field_in, cosine_lookup, sine_lookup):
    half_size = field_in.shape[-1] // 2
    first_half = field_in[..., :half_size]
    second_half = field_in[..., half_size:]
    return jnp.concatenate(
        [
            first_half * cosine_lookup + second_half * sine_lookup,
            second_half * cosine_lookup - first_half * sine_lookup,
        ],
        axis=-1,
    )


def mask_block(row_start, block_rows, seg_ids):
    length = seg_ids.shape[0]
    row_pos = row_start + jnp.arange(block_rows, dtype=jnp.int32)
    key_pos = jnp.arange(length, dtype=jnp.int32)
    return (key_pos[None, :] <= row_pos[:, None]) & (seg_ids[None, :] == seg_ids[:, None])


def block_scores(query_blk, key_heads, row_start, seg_ids):
    scores = (
        jnp.einsum("qhgd,khd->hgqk", query_blk, key_heads, preferred_element_type=jnp.float32)
        * ATTN_SCALE
    )
    allowed = mask_block(row_start, query_blk.shape[0], seg_ids)
    return jnp.where(allowed, scores, NEG_FILL)


def attend_block(query_blk, key_heads, value_head_rows, row_start, seg_ids):
    scores = block_scores(query_blk, key_heads, row_start, seg_ids)
    top_score = jnp.max(scores, axis=-1, keepdims=True)
    exp_total = jnp.sum(jnp.exp(scores - top_score), axis=-1, keepdims=True)
    log_total = top_score + jnp.log(exp_total)
    weights_soft = jnp.exp(scores - log_total).astype(jnp.bfloat16)
    mixed_heads = jnp.einsum(
        "hgqk,khd->qhgd", weights_soft, value_head_rows, preferred_element_type=jnp.float32
    )
    return (mixed_heads.astype(jnp.bfloat16), log_total[..., 0])


def attend_back(
    query_blk, key_heads, value_head_rows, log_total, grad_blk, mixed_blk, row_start, seg_ids
):
    scores = block_scores(query_blk, key_heads, row_start, seg_ids)
    weights_soft = jnp.exp(scores - log_total[..., None])
    row_delta = jnp.einsum(
        "qhgd,qhgd->hgq", grad_blk, mixed_blk, preferred_element_type=jnp.float32
    )
    grad_soft = jnp.einsum(
        "qhgd,khd->hgqk", grad_blk, value_head_rows, preferred_element_type=jnp.float32
    )
    grad_scores = (weights_soft * (grad_soft - row_delta[..., None]) * ATTN_SCALE).astype(
        jnp.bfloat16
    )
    grad_queries = jnp.einsum(
        "hgqk,khd->qhgd", grad_scores, key_heads, preferred_element_type=jnp.float32
    )
    key_gradient = jnp.einsum(
        "hgqk,qhgd->khd", grad_scores, query_blk, preferred_element_type=jnp.float32
    )
    value_gradient = jnp.einsum(
        "hgqk,qhgd->khd",
        weights_soft.astype(jnp.bfloat16),
        grad_blk,
        preferred_element_type=jnp.float32,
    )
    return (grad_queries, key_gradient, value_gradient)


def route_index(route_blk, expert_count, capacity):
    flat_routes = route_blk.reshape(-1)
    onehot = (flat_routes[:, None] == jnp.arange(expert_count, dtype=jnp.int32)[None, :]).astype(
        jnp.int32
    )
    earlier = jnp.cumsum(onehot, axis=0) - onehot
    slot_rank = jnp.sum(earlier * onehot, axis=1)
    return flat_routes * capacity + slot_rank


def body(
    activations,
    segments,
    routes,
    route_weights,
    norm_attn_gain,
    norm_ffn_gain,
    query_weight,
    key_matrix,
    value_matrix,
    output_projection_weight,
    expert_gate,
    expert_up,
    expert_down,
    grad_output,
):
    tensor_rank = lax.axis_index("tensor")
    tok_rows = activations.shape[0]
    model_width = activations.shape[1]
    experts_here = expert_gate.shape[0]
    expert_count = experts_here * lax.axis_size("expert")
    top_count = routes.shape[1]
    capacity = 2 * tok_rows * top_count // expert_count
    seg_ids = segments[0]
    length = seg_ids.shape[0]
    heads_q = query_weight.shape[1] // HEAD_DIM
    heads_kv = key_matrix.shape[1] // HEAD_DIM
    group_factor = heads_q // heads_kv
    block_rows = min(512, length)
    blocks = length // block_rows
    cosine_lookup, sine_lookup = rope_tables(length, HEAD_DIM)
    own_start = tensor_rank * tok_rows
    full_acts = lax.all_gather(activations, "tensor", axis=0, tiled=True)
    x_in = full_acts.astype(jnp.float32)
    normed_one, scale_one = norm_forward(x_in, norm_attn_gain)
    hidden_first = normed_one.astype(jnp.bfloat16)
    query_unrotated = jnp.dot(
        hidden_first, query_weight, preferred_element_type=jnp.float32
    ).reshape(length, heads_q, HEAD_DIM)
    query_head_rows = (
        apply_rotary(query_unrotated, cosine_lookup, sine_lookup)
        .astype(jnp.bfloat16)
        .reshape(length, heads_kv, group_factor, HEAD_DIM)
    )
    key_unrotated = jnp.dot(hidden_first, key_matrix, preferred_element_type=jnp.float32).reshape(
        length, heads_kv, HEAD_DIM
    )
    key_heads = apply_rotary(key_unrotated, cosine_lookup, sine_lookup).astype(jnp.bfloat16)
    value_head_rows = (
        jnp.dot(hidden_first, value_matrix, preferred_element_type=jnp.float32)
        .astype(jnp.bfloat16)
        .reshape(length, heads_kv, HEAD_DIM)
    )
    query_blocks = query_head_rows.reshape(blocks, block_rows, heads_kv, group_factor, HEAD_DIM)
    starts = jnp.arange(blocks, dtype=jnp.int32) * block_rows

    def forward_block(block_pair):
        return attend_block(block_pair[0], key_heads, value_head_rows, block_pair[1], seg_ids)

    mixed_heads, log_total = lax.map(forward_block, (query_blocks, starts))
    mixed_flat = mixed_heads.reshape(length, heads_q * HEAD_DIM)
    attn_part = jnp.dot(mixed_flat, output_projection_weight, preferred_element_type=jnp.float32)
    attn_out = lax.psum(attn_part, "tensor")
    residual = x_in + attn_out
    normed_two, scale_two = norm_forward(residual, norm_ffn_gain)
    h_two = normed_two.astype(jnp.bfloat16)
    h_own = lax.dynamic_slice_in_dim(h_two, own_start, tok_rows, 0)
    resid_own = lax.dynamic_slice_in_dim(residual, own_start, tok_rows, 0)
    slot_index = route_index(routes, expert_count, capacity)
    buffer = (
        jnp.zeros((expert_count * capacity, model_width), jnp.bfloat16)
        .at[slot_index]
        .set(jnp.repeat(h_own, top_count, axis=0))
        .reshape(expert_count, capacity, model_width)
    )
    received = lax.all_to_all(buffer, "expert", split_axis=0, concat_axis=1, tiled=True)
    gate_full, up_full, down_full = (expert_gate, expert_up, expert_down)
    rows_in = lax.all_gather(received, "tensor", axis=1, tiled=True)
    pre_gate = jnp.einsum("erd,edf->erf", rows_in, gate_full, preferred_element_type=jnp.float32)
    pre_up = jnp.einsum("erd,edf->erf", rows_in, up_full, preferred_element_type=jnp.float32)
    activated = (jax.nn.silu(pre_gate) * pre_up).astype(jnp.bfloat16)
    expert_part = jnp.einsum(
        "erf,efd->erd", activated, down_full, preferred_element_type=jnp.float32
    )
    expert_total = lax.psum_scatter(
        expert_part.astype(jnp.bfloat16), "tensor", scatter_dimension=1, tiled=True
    )
    returned = lax.all_to_all(expert_total, "expert", split_axis=1, concat_axis=0, tiled=True)
    picked = returned.reshape(-1, model_width)[slot_index].reshape(tok_rows, top_count, model_width)
    expert_mix = jnp.sum(route_weights[:, :, None] * picked.astype(jnp.float32), axis=1)
    block_out = (resid_own + expert_mix).astype(jnp.bfloat16)
    upstream_own = grad_output.astype(jnp.float32)
    grad_copies = (
        (route_weights[:, :, None] * upstream_own[:, None, :])
        .astype(jnp.bfloat16)
        .reshape(-1, model_width)
    )
    grad_buffer = (
        jnp.zeros((expert_count * capacity, model_width), jnp.bfloat16)
        .at[slot_index]
        .set(grad_copies)
        .reshape(expert_count, capacity, model_width)
    )
    grad_received = lax.all_to_all(grad_buffer, "expert", split_axis=0, concat_axis=1, tiled=True)
    grad_rows_in = lax.all_gather(grad_received, "tensor", axis=1, tiled=True)
    grad_down = jnp.einsum(
        "erf,erd->efd", activated, grad_rows_in, preferred_element_type=jnp.float32
    )
    grad_act = jnp.einsum(
        "erd,efd->erf", grad_rows_in, down_full, preferred_element_type=jnp.float32
    )
    gate_sigmoid = jax.nn.sigmoid(pre_gate)
    grad_pre_gate = (
        grad_act * pre_up * gate_sigmoid * (1.0 + pre_gate * (1.0 - gate_sigmoid))
    ).astype(jnp.bfloat16)
    grad_pre_up = (grad_act * pre_gate * gate_sigmoid).astype(jnp.bfloat16)
    grad_gate = jnp.einsum(
        "erd,erf->edf", rows_in, grad_pre_gate, preferred_element_type=jnp.float32
    )
    grad_up = jnp.einsum("erd,erf->edf", rows_in, grad_pre_up, preferred_element_type=jnp.float32)
    grad_in_part = jnp.einsum(
        "erf,edf->erd", grad_pre_gate, gate_full, preferred_element_type=jnp.float32
    ) + jnp.einsum("erf,edf->erd", grad_pre_up, up_full, preferred_element_type=jnp.float32)
    grad_in_rows = lax.psum_scatter(grad_in_part, "tensor", scatter_dimension=1, tiled=True)
    grad_back = lax.all_to_all(
        grad_in_rows.astype(jnp.bfloat16), "expert", split_axis=1, concat_axis=0, tiled=True
    )
    picked_grad = grad_back.reshape(-1, model_width)[slot_index].reshape(
        tok_rows, top_count, model_width
    )
    grad_h_own = jnp.sum(route_weights[:, :, None] * picked_grad.astype(jnp.float32), axis=1)
    upstream_full, grad_h_full = (
        lax.all_gather(upstream_own, "tensor", axis=0, tiled=True),
        lax.all_gather(grad_h_own, "tensor", axis=0, tiled=True),
    )
    grad_norm_part, grad_ffn_gain = norm_backward(residual, scale_two, norm_ffn_gain, grad_h_full)
    grad_resid = upstream_full + grad_norm_part
    residual_gradient_second = grad_resid.astype(jnp.bfloat16)
    grad_mix_w = jnp.einsum(
        "sa,sb->ab", mixed_flat, residual_gradient_second, preferred_element_type=jnp.float32
    )
    mixed_gradient = (
        jnp.einsum(
            "im,dm->id",
            residual_gradient_second,
            output_projection_weight,
            preferred_element_type=jnp.float32,
        )
        .astype(jnp.bfloat16)
        .reshape(blocks, block_rows, heads_kv, group_factor, HEAD_DIM)
    )

    def backward_block(block_pack):
        return attend_back(
            block_pack[0],
            key_heads,
            value_head_rows,
            block_pack[1],
            block_pack[2],
            block_pack[3],
            block_pack[4],
            seg_ids,
        )

    grad_queries, key_gradient, value_gradient = lax.map(
        backward_block, (query_blocks, log_total, mixed_gradient, mixed_heads, starts)
    )
    key_gradient = jnp.sum(key_gradient, axis=0)
    value_gradient = jnp.sum(value_gradient, axis=0)
    grad_q_rows = (
        invert_rotary(grad_queries.reshape(length, heads_q, HEAD_DIM), cosine_lookup, sine_lookup)
        .astype(jnp.bfloat16)
        .reshape(length, heads_q * HEAD_DIM)
    )
    grad_key_rows = (
        invert_rotary(key_gradient, cosine_lookup, sine_lookup)
        .astype(jnp.bfloat16)
        .reshape(length, heads_kv * HEAD_DIM)
    )
    grad_value_rows = value_gradient.astype(jnp.bfloat16).reshape(length, heads_kv * HEAD_DIM)
    grad_q_w = jnp.einsum(
        "sd,sa->da", hidden_first, grad_q_rows, preferred_element_type=jnp.float32
    )
    grad_k_w = jnp.einsum(
        "sd,sa->da", hidden_first, grad_key_rows, preferred_element_type=jnp.float32
    )
    grad_v_w = jnp.einsum(
        "sd,sa->da", hidden_first, grad_value_rows, preferred_element_type=jnp.float32
    )
    grad_h_part = (
        jnp.einsum("sa,da->sd", grad_q_rows, query_weight, preferred_element_type=jnp.float32)
        + jnp.einsum("sa,da->sd", grad_key_rows, key_matrix, preferred_element_type=jnp.float32)
        + jnp.einsum("sa,da->sd", grad_value_rows, value_matrix, preferred_element_type=jnp.float32)
    )
    grad_h_one = lax.psum(grad_h_part, "tensor")
    grad_x_part, grad_attn_gain = norm_backward(x_in, scale_one, norm_attn_gain, grad_h_one)
    grad_full = grad_resid + grad_x_part
    grad_input = lax.dynamic_slice_in_dim(grad_full, own_start, tok_rows, 0)
    dense_sums = lax.psum(
        (grad_attn_gain, grad_ffn_gain, grad_q_w, grad_k_w, grad_v_w, grad_mix_w), ("dp", "expert")
    )
    gate_half, up_half, down_half = (grad_gate, grad_up, grad_down)
    gate_sum, up_sum, down_sum = lax.psum((gate_half, up_half, down_half), "dp")
    return (
        block_out,
        grad_input,
        dense_sums[0],
        dense_sums[1],
        dense_sums[2],
        dense_sums[3],
        dense_sums[4],
        dense_sums[5],
        gate_sum,
        up_sum,
        down_sum,
    )


def solution(mesh):
    placed = (
        P(("dp", "expert", "tensor"), None),
        P(("dp", "expert"), None),
        P(("dp", "expert", "tensor"), None),
        P(("dp", "expert", "tensor"), None),
        P(),
        P(),
        P(None, "tensor"),
        P(None, "tensor"),
        P(None, "tensor"),
        P("tensor", None),
        P("expert", None, "tensor"),
        P("expert", None, "tensor"),
        P("expert", "tensor", None),
        P(("dp", "expert", "tensor"), None),
    )
    return jax.shard_map(
        body,
        mesh=mesh,
        in_specs=placed,
        out_specs=(
            P(("dp", "expert", "tensor"), None),
            P(("dp", "expert", "tensor"), None),
            P(),
            P(),
            P(None, "tensor"),
            P(None, "tensor"),
            P(None, "tensor"),
            P("tensor", None),
            P("expert", None, "tensor"),
            P("expert", None, "tensor"),
            P("expert", "tensor", None),
        ),
        check_vma=False,
    )
```

profile of v0, /device:TPU:0, one launch (start us, length us, event | category | flops | bytes accessed | tf_op | source)
XLA Modules:
  0.0 1433.7 jit_solution(16432259173664442176)
XLA Ops:
  16.2 9.6 scatter_custom_fusion.1
  47.8 123.7 %all-to-all-done.2 = bf16[16,128,1536]{2,1,0:T(8,128)(2,1)} async-done(((bf16[16,128,1536]{2,1,0:T(8,128)(2,1)}), bf16[16,128,1536]{2,1,0:T(8,128)(2,1)}, u32[]{:S(2)}, u32[]{:S(2)}) %all-to-all-start.2) | async-done | bytes 6291488 | tf_op jit(solution)/shard_map/all_to_all | solution.py:231
  180.6 9.9 scatter_custom_fusion
  190.5 142.7 %all_to_all.66 = bf16[16,128,1536]{2,1,0:T(8,128)(2,1)S(1)} all-to-all(bf16[16,128,1536]{2,1,0:T(8,128)(2,1)} %bitcast.164), channel_id=1, replica_groups=mesh['dp'=2,'expert'=8,'tensor'=2] {'expert'}, dimensions={0} | all-to-all | bytes 12582912 | tf_op jit(solution)/shard_map/all_to_all | solution.py:203
  336.6 11.0 fusion.61
  347.6 12.6 all-gather.5.cloned.1.call-done
  367.3 9.4 multiply_convert_fusion.2
  384.8 19.7 %fusion.62 = f32[2,2048,1536]{2,1,0:T(8,128)} fusion(bf16[2,2048,256]{2,1,0:T(8,128)(2,1)} %get-tuple-element.84, bf16[2,1536,256]{2,1,0:T(8,128)(2,1)} %param.24), kind=kOutput, calls=%fused_computation.122 | convolution fusion | flops 3221225472 | bytes 28835840 | tf_op jit(solution)/shard_map/erf,edf->erd/dot_general | solution.py:248
  404.6 21.5 %convolution_add_fusion = f32[2,2048,1536]{2,1,0:T(8,128)} fusion(f32[2,2048,1536]{2,1,0:T(8,128)} %fusion.62, bf16[2,2048,256]{2,1,0:T(8,128)(2,1)} %get-tuple-element.85, bf16[2,1536,256]{2,1,0:T(8,128)(2,1)} %param.25), kind=kOutput, calls=%fused_computation.4 | convolution fusion | flops 3227516928 | bytes 54001664 | tf_op jit(solution)/shard_map/erf,edf->erd/dot_general | solution.py:250
  426.1 12.8 copy.74
  444.7 18.1 %reduce-scatter.5.cloned.1.call-done = f32[2,1024,1536]{2,1,0:T(8,128)} async-done(((f32[2,2048,1536]{2,1,0:T(8,128)}), f32[2,1024,1536]{2,1,0:T(8,128)}) %reduce-scatter.5.cloned.1.call-update) | async-done | bytes 12582928 | tf_op jit(solution)/shard_map/reduce_scatter | solution.py:251
  462.8 8.0 convert_element_type.120
  470.8 12.7 copy.78
  483.6 99.8 %all-to-all-done.1 = bf16[2,1024,1536]{2,0,1:T(2,128)(2,1)} async-done(((bf16[2,1024,1536]{2,0,1:T(2,128)(2,1)}), bf16[2,1024,1536]{2,0,1:T(2,128)(2,1)}, u32[]{:S(2)}, u32[]{:S(2)}) %all-to-all-start.1) | async-done | bytes 6291488 | tf_op jit(solution)/shard_map/all_to_all | solution.py:215
  595.1 10.9 gather_fusion
  606.0 119.9 %all-to-all-done.3 = bf16[2,1024,1536]{2,0,1:T(2,128)(2,1)} async-done(((bf16[2,1024,1536]{2,0,1:T(2,128)(2,1)}), bf16[2,1024,1536]{2,0,1:T(2,128)(2,1)}, u32[]{:S(2)}, u32[]{:S(2)}) %all-to-all-start.3) | async-done | bytes 6291488 | tf_op jit(solution)/shard_map/all_to_all | solution.py:252
  732.5 10.9 gather_fusion.1
  743.4 8.7 fusion
  753.1 12.2 fusion.64
  790.1 11.8 fusion.65
  801.9 10.4 fusion.66
  829.9 78.4 %all-reduce = (f32[1536]{0:T(1024)}, f32[1536]{0:T(1024)}) all-reduce(f32[1536]{0:T(1024)S(1)} %get-tuple-element.56, f32[1536]{0:T(1024)S(1)} %copy-done.51), channel_id=1, replica_groups=mesh['dp'=2,'expert'=8,'tensor'=2] {'dp','expert'}, use_global_device_ids=true, to_apply=%region_18.19 | all-reduce | flops 3072 | bytes 24576 | tf_op jit(solution)/shard_map/psum | solution.py:326
  911.0 126.9 %all-reduce.14.cloned.1.call-done = (f32[2,1536,256]{2,1,0:T(8,128)}, f32[2,1536,256]{2,1,0:T(8,128)}, f32[2,256,1536]{2,1,0:T(8,128)}) async-done(((f32[2,1536,256]{2,1,0:T(8,128)}, f32[2,1536,256]{2,1,0:T(8,128)}, f32[2,256,1536]{2,1,0:T(8,128)}), (f32[2,1536,256]{2,1,0:T(8,128)}, f32[2,1536,256]{2,1,0:T(8,128)}, f32[2,256,1536]{2,1,0:T(8,128)})) %all-reduce.14.cloned.1.call-update) | async-done | bytes 9437200 | tf_op jit(solution)/shard_map/psum | solution.py:330
  1037.9 368.8 %all-reduce.12.cloned.1.call-done = (f32[1536,768]{1,0:T(8,128)}, f32[1536,256]{1,0:T(8,128)}, f32[1536,256]{1,0:T(8,128)}, f32[768,1536]{1,0:T(8,128)}) async-done(((f32[1536,768]{1,0:T(8,128)}, f32[1536,256]{1,0:T(8,128)}, f32[1536,256]{1,0:T(8,128)}, f32[768,1536]{1,0:T(8,128)}), (f32[1536,768]{1,0:T(8,128)}, f32[1536,256]{1,0:T(8,128)}, f32[1536,256]{1,0:T(8,128)}, ...) | async-done | bytes 12582928 | tf_op jit(solution)/shard_map/psum | solution.py:326
  (229 shorter events, 148.0 us)
Async XLA Ops:
  7.2 38.6 %copy-start = (bf16[768,1536]{1,0:T(8,128)(2,1)S(1)}, bf16[768,1536]{1,0:T(8,128)(2,1)}, u32[]{:S(2)}) copy-start(bf16[768,1536]{1,0:T(8,128)(2,1)} %param.23) | copy-start | bytes 7077892
  15.2 10.6 copy-start.8
  25.8 11.4 copy-start.54
  25.8 11.5 copy-start.40
  25.8 145.6 %all-to-all-start.2 = ((bf16[16,128,1536]{2,1,0:T(8,128)(2,1)}), bf16[16,128,1536]{2,1,0:T(8,128)(2,1)}, u32[]{:S(2)}, u32[]{:S(2)}) async-start(bf16[16,128,1536]{2,1,0:T(8,128)(2,1)} %bitcast.162), calls=%async_computation.3 | async-start | bytes 12582912 | tf_op jit(solution)/shard_map/all_to_all | solution.py:231
  33.3 144.3 %all-reduce.8.cloned.1.call-start = ((), (), s32[]{:S(2)}) async-start(), calls=%async_computation.6 | async-start | bytes 3145728 | tf_op jit(solution)/shard_map/psum | solution.py:190
  33.3 5.9 copy-start.20
  36.2 141.4 %copy-start.1 = (bf16[256,1536]{1,0:T(8,128)(2,1)}, bf16[256,1536]{1,0:T(8,128)(2,1)S(1)}, u32[]{:S(2)}) copy-start(bf16[256,1536]{1,0:T(8,128)(2,1)S(1)} %all_gather.15) | copy-start | bytes 2359300
  37.4 6.8 copy-start.46
  47.7 288.9 %all-gather.9.cloned.1.call-start = ((), (), s32[]{:S(2)}) async-start(), calls=%async_computation.10 | async-start | bytes 18874368 | tf_op jit(solution)/shard_map/all_gather | solution.py:232
  177.5 182.7 %all-gather.5.cloned.1.call-start = ((), (), s32[]{:S(2)}) async-start(), calls=%async_computation.7 | async-start | bytes 18874368 | tf_op jit(solution)/shard_map/all_gather | solution.py:205
  336.6 89.5 %reduce-scatter.3.cloned.1.call-start = ((), (), s32[]{:S(2)}) async-start(), calls=%async_computation.8 | async-start | bytes 18874368 | tf_op jit(solution)/shard_map/reduce_scatter | solution.py:212
  360.2 7.0 copy-start.22
  360.2 7.0 copy-start.58
  367.2 10.8 copy-start.25
  384.4 78.4 %reduce-scatter.5.cloned.1.call-start = ((), (), s32[]{:S(2)}) async-start(), calls=%async_computation.11 | async-start | bytes 37748736 | tf_op jit(solution)/shard_map/reduce_scatter | solution.py:251
  438.9 144.5 %all-to-all-start.1 = ((bf16[2,1024,1536]{2,0,1:T(2,128)(2,1)}), bf16[2,1024,1536]{2,0,1:T(2,128)(2,1)}, u32[]{:S(2)}, u32[]{:S(2)}) async-start(bf16[2,1024,1536]{2,0,1:T(2,128)(2,1)} %copy.74), calls=%async_computation.2 | async-start | bytes 12582912 | tf_op jit(solution)/shard_map/all_to_all | solution.py:215
  583.4 142.5 %all-to-all-start.3 = ((bf16[2,1024,1536]{2,0,1:T(2,128)(2,1)}), bf16[2,1024,1536]{2,0,1:T(2,128)(2,1)}, u32[]{:S(2)}, u32[]{:S(2)}) async-start(bf16[2,1024,1536]{2,0,1:T(2,128)(2,1)} %copy.78), calls=%async_computation.5 | async-start | bytes 12582912 | tf_op jit(solution)/shard_map/all_to_all | solution.py:252
  588.1 177.2 %all-gather.11.cloned.1.call-start = ((), (), s32[]{:S(2)}) async-start(), calls=%async_computation.12 | async-start | bytes 2359296 | tf_op jit(solution)/shard_map/all_gather | solution.py:261
  752.1 22.2 %all-gather.7.cloned.1.call-start = ((), (), s32[]{:S(2)}) async-start(), calls=%async_computation.9 | async-start | bytes 2359296 | tf_op jit(solution)/shard_map/all_gather | solution.py:260
  752.9 74.1 %all-reduce.10.cloned.1.call-start = ((), (), s32[]{:S(2)}) async-start(), calls=%async_computation.13 | async-start | bytes 3145728 | tf_op jit(solution)/shard_map/psum | solution.py:322
  789.8 248.1 %all-reduce.14.cloned.1.call-start = ((), (), s32[]{:S(2)}) async-start(), calls=%async_computation.15 | async-start | bytes 18874368 | tf_op jit(solution)/shard_map/psum | solution.py:330
  812.4 594.3 %all-reduce.12.cloned.1.call-start = ((), (), s32[]{:S(2)}) async-start(), calls=%async_computation.14 | async-start | bytes 25165824 | tf_op jit(solution)/shard_map/psum | solution.py:326
  1406.7 6.1 copy-start.23
  (48 other events, 103.7 us)
Sparse Core Ops, SparseCore 0:
  47.9 21.7 all-reduce.7
  177.6 23.4 all-gather.8
  336.7 23.4 all-gather.4
  384.5 22.6 reduce-scatter.2
  426.2 36.6 reduce-scatter.4
  752.3 8.7 all-gather.10
  763.3 10.9 all-gather.6
  789.9 21.5 all-reduce.9
  814.7 223.1 all-reduce.13
  1044.8 361.8 all-reduce.11
where the time goes:
time: 1440 us; the launch traced here: 1430 us
  waiting for transfers between devices  877 us (61%)
  blocking collectives  224 us (16%)
  matrix products  135 us (9%)
  local copies, waits for them, and re-layouts  112 us (8%)
  other arithmetic  50.5 us (4%)
  starting transfers between devices  19.4 us (1%)
  between operations  15.4 us (1%)
    psum x1, waiting for transfers between devices, body(): lax.psum((grad_attn_gain, grad_ffn_gain, grad_q_w, grad_k_w, grad_v_w, gr...  369 us
    all_to_all x1, blocking collectives, body(): lax.all_to_all(buffer, 'expert', split_axis=0, concat_axis=1, tiled=True)  143 us
    psum x1, waiting for transfers between devices, body(): gate_sum, up_sum, down_sum = lax.psum((gate_half, up_half, down_half), 'dp')  127 us
    all_to_all x1, waiting for transfers between devices, body(): lax.all_to_all(grad_buffer, 'expert', split_axis=0, concat_axis=1, tiled=...  124 us
    all_to_all x1, waiting for transfers between devices, body(): lax.all_to_all(grad_in_rows.astype(jnp.bfloat16), 'expert', split_axis=1,...  120 us
    all_to_all x1, waiting for transfers between devices, body(): lax.all_to_all(expert_total, 'expert', split_axis=1, concat_axis=0, tiled...  99.8 us
    psum x1, blocking collectives, body(): lax.psum((grad_attn_gain, grad_ffn_gain, grad_q_w, grad_k_w, grad_v_w, gr...  78.4 us
    unnamed x127, local copies, waits for them, and re-layouts  31.3 us
  transfers between devices with their start and end apart: 13, of which 8 were waited for; matrix products, arithmetic and copies ran while one was open for 13% of the time, Pallas kernels for 0%

commit v1 on v0

v1 whole, which is shorter than its diff:
```python
import jax
import jax.numpy as jnp
from jax import lax
from jax.sharding import PartitionSpec as P

HEAD_DIM = 64
EPS = 1e-05
ATTN_SCALE = 0.015625
THETA = 10000.0
NEG_FILL = -1e30
F32 = jnp.float32
BF16 = jnp.bfloat16


def swap(values):
    return lax.ppermute(values, "tensor", [(0, 1), (1, 0)])


def norm_forward(values, gain_vector):
    inv_scale = lax.rsqrt(jnp.mean(values * values, axis=-1, keepdims=True) + EPS)
    return (values * inv_scale * gain_vector, inv_scale)


def norm_backward(values, inv_scale, gain_vector, upstream):
    weighted = upstream * gain_vector
    inner = jnp.mean(weighted * values, axis=-1, keepdims=True)
    value_gradient = inv_scale * weighted - values * (inv_scale * inv_scale * inv_scale) * inner
    grad_gain = jnp.sum(upstream * values * inv_scale, axis=0)
    return (value_gradient, grad_gain)


def rope_tables(position):
    frequency = THETA ** (-jnp.arange(HEAD_DIM // 2, dtype=F32) * 2.0 / HEAD_DIM)
    angle_table = position.astype(F32)[:, None] * frequency[None, :]
    return (jnp.cos(angle_table)[:, None, :], jnp.sin(angle_table)[:, None, :])


def rotate(field_in, cosine, sine):
    first, second = jnp.split(field_in, 2, axis=-1)
    return jnp.concatenate([first * cosine - second * sine, second * cosine + first * sine], axis=-1)


def dot(spec, left, right):
    return jnp.einsum(spec, left, right, preferred_element_type=F32)


def body(
    activations,
    segments,
    routes,
    route_weights,
    norm_attn_gain,
    norm_ffn_gain,
    query_weight,
    key_matrix,
    value_matrix,
    output_projection_weight,
    expert_gate,
    expert_up,
    expert_down,
    grad_output,
):
    tensor_rank = lax.axis_index("tensor")
    rows, width = activations.shape
    experts_here = expert_gate.shape[0]
    expert_count = experts_here * lax.axis_size("expert")
    length = segments.shape[1]
    heads_q = query_weight.shape[1] // HEAD_DIM
    heads_kv = key_matrix.shape[1] // HEAD_DIM
    group = heads_q // heads_kv

    position = (jnp.arange(length, dtype=jnp.int32) + tensor_rank * rows) % length
    seg_ids = jnp.where(tensor_rank == 0, segments[0], jnp.roll(segments[0], rows))
    cosine, sine = rope_tables(position)
    allowed = (position[None, :] <= position[:, None]) & (seg_ids[None, :] == seg_ids[:, None])

    gate = jnp.concatenate([expert_gate, swap(expert_gate)], axis=2)
    up = jnp.concatenate([expert_up, swap(expert_up)], axis=2)
    down = jnp.concatenate([expert_down, swap(expert_down)], axis=1)
    upstream_all = lax.all_gather(grad_output, "expert", axis=0, tiled=True)
    named = routes[:, :, None] == jnp.arange(expert_count, dtype=jnp.int32)
    weight_table = jnp.sum(jnp.where(named, route_weights[:, :, None], 0.0), axis=1)
    weights_all = lax.all_gather(weight_table, "expert", axis=0, tiled=True)
    first_expert = lax.axis_index("expert") * experts_here
    weights_here = lax.dynamic_slice_in_dim(weights_all, first_expert, experts_here, 1).T

    x_in = jnp.concatenate([activations, swap(activations)], axis=0).astype(F32)
    normed_one, scale_one = norm_forward(x_in, norm_attn_gain)
    hidden_first = normed_one.astype(BF16)
    queries = dot("td,da->ta", hidden_first, query_weight).reshape(length, heads_q, HEAD_DIM)
    queries = rotate(queries, cosine, sine).astype(BF16).reshape(length, heads_kv, group, HEAD_DIM)
    keys = dot("td,da->ta", hidden_first, key_matrix).reshape(length, heads_kv, HEAD_DIM)
    keys = rotate(keys, cosine, sine).astype(BF16)
    value_rows = dot("td,da->ta", hidden_first, value_matrix).astype(BF16)
    value_rows = value_rows.reshape(length, heads_kv, HEAD_DIM)
    scores = jnp.where(allowed, dot("qhgd,khd->hgqk", queries, keys) * ATTN_SCALE, NEG_FILL)
    top_score = jnp.max(scores, axis=-1, keepdims=True)
    log_total = top_score + jnp.log(jnp.sum(jnp.exp(scores - top_score), axis=-1, keepdims=True))
    mixed = dot("hgqk,khd->qhgd", jnp.exp(scores - log_total).astype(BF16), value_rows).astype(BF16)
    mixed_flat = mixed.reshape(length, heads_q * HEAD_DIM)
    attn_part = dot("ta,ad->td", mixed_flat, output_projection_weight)
    residual = x_in[:rows] + attn_part[:rows] + swap(attn_part[rows:])
    normed_two, scale_two = norm_forward(residual, norm_ffn_gain)
    tokens_in = lax.all_gather(normed_two.astype(BF16), "expert", axis=0, tiled=True)

    pre_gate = dot("td,edf->etf", tokens_in, gate)
    pre_up = dot("td,edf->etf", tokens_in, up)
    gate_sigmoid = jax.nn.sigmoid(pre_gate)
    activated = (pre_gate * gate_sigmoid * pre_up).astype(BF16)
    expert_out = dot("etf,efd->etd", activated, down).astype(BF16)
    mix_part = jnp.sum(weights_here[:, :, None] * expert_out.astype(F32), axis=0).astype(BF16)
    grad_rows = (weights_here[:, :, None] * upstream_all.astype(F32)[None]).astype(BF16)
    grad_act = dot("etd,efd->etf", grad_rows, down)
    grad_pre_gate = (
        grad_act * pre_up * gate_sigmoid * (1.0 + pre_gate * (1.0 - gate_sigmoid))
    ).astype(BF16)
    grad_pre_up = (grad_act * pre_gate * gate_sigmoid).astype(BF16)
    grad_in = dot("etf,edf->etd", grad_pre_gate, gate) + dot("etf,edf->etd", grad_pre_up, up)
    grad_part = jnp.sum(weights_here[:, :, None] * grad_in, axis=0).astype(BF16)
    grad_h_own = lax.psum_scatter(grad_part, "expert", scatter_dimension=0, tiled=True)
    expert_mix = lax.psum_scatter(mix_part, "expert", scatter_dimension=0, tiled=True)
    block_out = (residual + expert_mix.astype(F32)).astype(BF16)

    def expert_sum(whole, axis):
        own, other = jnp.split(whole, 2, axis=axis)
        half = own + swap(other.astype(BF16)).astype(F32)
        return lax.psum(half.astype(BF16), "dp").astype(F32)

    gate_sum = expert_sum(dot("td,etf->edf", tokens_in, grad_pre_gate), 2)
    up_sum = expert_sum(dot("td,etf->edf", tokens_in, grad_pre_up), 2)
    down_sum = expert_sum(dot("etf,etd->efd", activated, grad_rows), 1)

    upstream_own = grad_output.astype(F32)
    grad_norm_part, grad_ffn_gain = norm_backward(
        residual, scale_two, norm_ffn_gain, grad_h_own.astype(F32)
    )
    grad_resid = upstream_own + grad_norm_part
    resid_own = grad_resid.astype(BF16)
    resid_full = jnp.concatenate([resid_own, swap(resid_own)], axis=0)
    grad_mix_w = dot("sa,sb->ab", mixed_flat, resid_full)
    mixed_grad = dot("im,dm->id", resid_full, output_projection_weight).astype(BF16)
    mixed_grad = mixed_grad.reshape(length, heads_kv, group, HEAD_DIM)
    probs = jnp.exp(scores - log_total)
    row_delta = dot("qhgd,qhgd->hgq", mixed_grad, mixed)
    grad_soft = dot("qhgd,khd->hgqk", mixed_grad, value_rows)
    grad_scores = (probs * (grad_soft - row_delta[..., None]) * ATTN_SCALE).astype(BF16)
    grad_queries = dot("hgqk,khd->qhgd", grad_scores, keys)
    grad_keys = dot("hgqk,qhgd->khd", grad_scores, queries)
    grad_values = dot("hgqk,qhgd->khd", probs.astype(BF16), mixed_grad)
    grad_q_rows = rotate(grad_queries.reshape(length, heads_q, HEAD_DIM), cosine, -sine)
    grad_q_rows = grad_q_rows.astype(BF16).reshape(length, -1)
    grad_k_rows = rotate(grad_keys, cosine, -sine).astype(BF16).reshape(length, -1)
    grad_v_rows = grad_values.astype(BF16).reshape(length, -1)
    grad_q_w = dot("sd,sa->da", hidden_first, grad_q_rows)
    grad_k_w = dot("sd,sa->da", hidden_first, grad_k_rows)
    grad_v_w = dot("sd,sa->da", hidden_first, grad_v_rows)
    grad_h_part = (
        dot("sa,da->sd", grad_q_rows, query_weight)
        + dot("sa,da->sd", grad_k_rows, key_matrix)
        + dot("sa,da->sd", grad_v_rows, value_matrix)
    )
    grad_h_one = grad_h_part[:rows] + swap(grad_h_part[rows:])
    grad_x_part, grad_attn_gain = norm_backward(
        x_in[:rows], scale_one[:rows], norm_attn_gain, grad_h_one
    )
    grad_input = grad_resid + grad_x_part
    dense = [t.astype(BF16) for t in (grad_q_w, grad_k_w, grad_v_w, grad_mix_w)]
    dense = [t.astype(F32) for t in lax.psum(dense, ("dp", "expert"))]
    gains = lax.psum(jnp.stack([grad_attn_gain, grad_ffn_gain]), ("dp", "expert", "tensor"))
    return (
        block_out,
        grad_input,
        gains[0],
        gains[1],
        *dense,
        gate_sum,
        up_sum,
        down_sum,
    )


def solution(mesh):
    tokens = P(("dp", "expert", "tensor"), None)
    whole = P()
    columns = P(None, "tensor")
    hidden_last = P("expert", None, "tensor")
    hidden_mid = P("expert", "tensor", None)
    mixer = P("tensor", None)
    return jax.shard_map(
        body,
        mesh=mesh,
        in_specs=(
            tokens,
            P(("dp", "expert"), None),
            tokens,
            tokens,
            whole,
            whole,
            columns,
            columns,
            columns,
            mixer,
            hidden_last,
            hidden_last,
            hidden_mid,
            tokens,
        ),
        out_specs=(
            tokens,
            tokens,
            whole,
            whole,
            columns,
            columns,
            columns,
            mixer,
            hidden_last,
            hidden_last,
            hidden_mid,
        ),
        check_vma=False,
    )
```

time: 1440 us -> 698 us (0.48)
  waiting for transfers between devices: 877 us -> 435 us
  blocking collectives: 224 us -> 73.3 us
  local copies, waits for them, and re-layouts: 112 us -> 32.9 us
  matrix products: 135 us -> 89.9 us
  starting transfers between devices: 19.4 us -> 2.72 us
    all_to_all x3 -> x0, waiting for transfers between devices: 343 us -> none  [the longest x1 124 us: body(): lax.all_to_all(grad_buffer, 'expert', split_axis=0, concat_axis=1, tiled=...]
    psum x4 -> x2, waiting for transfers between devices: 496 us -> 305 us  [the longest x1 216 us: body(): dense = [t.astype(F32) for t in lax.psum(dense, ('dp', 'expert'))]]
    all_to_all x1 -> x0, blocking collectives: 143 us -> none  [body(): lax.all_to_all(buffer, 'expert', split_axis=0, concat_axis=1, tiled=True)]
    reduce_scatter x2, waiting for transfers between devices: 18.1 us -> 64.8 us  [the longest x1 40.9 us: body(): lax.psum_scatter(grad_part, 'expert', scatter_dimension=0, tiled=True)]
    dot_general x27, matrix products: 135 us -> 89.9 us  [dot(): return jnp.einsum(spec, left, right, preferred_element_type=F32)]
    all_gather x4 -> x2, waiting for transfers between devices: 18.7 us -> 60.8 us  [the longest x1 56.4 us: body(): lax.all_gather(normed_two.astype(BF16), 'expert', axis=0, tiled=True)]
    psum x1, blocking collectives: 78.4 us -> 41 us  [body(): lax.psum(jnp.stack([grad_attn_gain, grad_ffn_gain]), ('dp', 'expert', 'te...]
    all_gather x1, blocking collectives: 2.88 us -> 32.3 us  [body(): weights_all = lax.all_gather(weight_table, 'expert', axis=0, tiled=True)]
  transfers between devices with their start and end apart: 13 -> 16, of which waited for: 8 -> 8; matrix products, arithmetic and copies ran while one was open for 13% -> 16% of each run, Pallas kernels for 0% -> 0%
where the time goes in v1:
time: 698 us; the launch traced here: 691 us
  waiting for transfers between devices  435 us (62%)
  matrix products  89.9 us (13%)
  blocking collectives  73.3 us (11%)
  other arithmetic  41.7 us (6%)
  local copies, waits for them, and re-layouts  32.9 us (5%)
  between operations  15.2 us (2%)
    psum x1, waiting for transfers between devices, body(): dense = [t.astype(F32) for t in lax.psum(dense, ('dp', 'expert'))]  216 us
    dot_general x27, matrix products, dot(): return jnp.einsum(spec, left, right, preferred_element_type=F32)  89.9 us
    psum x1, waiting for transfers between devices, expert_sum(): return lax.psum(half.astype(BF16), 'dp').astype(F32)  88.5 us
    all_gather x1, waiting for transfers between devices, body(): lax.all_gather(normed_two.astype(BF16), 'expert', axis=0, tiled=True)  56.4 us
    psum x1, blocking collectives, body(): lax.psum(jnp.stack([grad_attn_gain, grad_ffn_gain]), ('dp', 'expert', 'te...  41 us
    reduce_scatter x1, waiting for transfers between devices, body(): lax.psum_scatter(grad_part, 'expert', scatter_dimension=0, tiled=True)  40.9 us
    all_gather x1, blocking collectives, body(): weights_all = lax.all_gather(weight_table, 'expert', axis=0, tiled=True)  32.3 us
    unnamed x143, local copies, waits for them, and re-layouts  23.9 us
  transfers between devices with their start and end apart: 16, of which 8 were waited for; matrix products, arithmetic and copies ran while one was open for 16% of the time, Pallas kernels for 0%

profile of v1, /device:TPU:0, one launch (start us, length us, event | category | flops | bytes accessed | tf_op | source)
XLA Modules:
  0.0 690.8 jit_solution(6405158610316332684)
XLA Ops:
  32.3 32.3 %all_gather.9 = f32[1024,16]{0,1:T(8,128)S(1)} all-gather(f32[128,16]{0,1:T(8,128)S(1)} %select_reduce_fusion), channel_id=1, replica_groups=mesh['dp'=2,'expert'=8,'tensor'=2] {'expert'}, dimensions={0}, use_global_device_ids=true | all-gather | bytes 73728 | tf_op jit(solution)/shard_map/all_gather | solution.py:83
  69.9 4.4 all-gather.5.cloned.1.call-done
  74.3 5.4 convert_element_type.165
  79.7 56.4 %all-gather.3.cloned.1.call-done = bf16[1024,1536]{1,0:T(8,128)(2,1)} async-done(((bf16[128,1536]{1,0:T(8,128)(2,1)}), bf16[1024,1536]{1,0:T(8,128)(2,1)}) %all-gather.3.cloned.1.call-update) | async-done | bytes 3145744 | tf_op jit(solution)/shard_map/all_gather | solution.py:104
  136.1 6.4 fusion.24
  142.5 6.5 fusion.26
  149.1 9.5 %fusion.9 = (bf16[2,1024,512]{1,2,0:T(8,128)(2,1)}, bf16[2,1024,512]{1,2,0:T(8,128)(2,1)}, bf16[2,1024,512]{1,2,0:T(8,128)(2,1)S(1)}) fusion(f32[2,512,1024]{2,1,0:T(8,128)S(1)} %fusion.24, f32[2,512,1024]{2,1,0:T(8,128)} %fusion.26, bf16[2,512,1536]{2,1,0:T(8,128)(2,1)} %constant_dynamic-update-slice_fusion, f32[1024,1536]{1,0:T(8,128)S(1)} %bitcast.160, ...), kind=kOutput, calls=%fused_computation.16 | convolution fusion | flops 3244294144 | bytes 24125440 | tf_op jit(solution)/shard_map/etd,efd->etf/dot_general | solution.py:44
  158.6 8.6 %fusion.30 = f32[2,1024,1536]{2,1,0:T(8,128)} fusion(bf16[2,1024,512]{1,2,0:T(8,128)(2,1)S(1)} %get-tuple-element.61, bf16[2,1536,256]{1,2,0:T(8,128)(2,1)} %collective-permute-done.3, bf16[2,1536,256]{1,2,0:T(8,128)(2,1)S(1)} %copy-done.11), kind=kOutput, calls=%fused_computation.59 | convolution fusion | flops 3227516928 | bytes 17825792 | tf_op jit(solution)/shard_map/etf,edf->etd/dot_general | solution.py:44
  167.2 13.0 %multiply_reduce_fusion = bf16[1024,1536]{1,0:T(8,128)(2,1)} fusion(f32[2,1024,1536]{2,1,0:T(8,128)} %fusion.30, f32[2,1024]{1,0:T(2,128)S(1)} %dynamic-slice_bitcast_fusion, bf16[2,1024,512]{1,2,0:T(8,128)(2,1)} %get-tuple-element.59, bf16[2,1536,256]{1,2,0:T(8,128)(2,1)} %collective-permute-done.2, bf16[2,1536,256]{1,2,0:T(8,128)(2,1)} %copy.77), kind=kOutput, calls=%fused_computation | convolution fusion | flops 3235381248 | bytes 20979712 | tf_op jit(solution)/shard_map/etf,edf->etd/dot_general | solution.py:44
  180.7 7.1 %fusion = f32[2,512,1536]{2,1,0:T(8,128)S(1)} fusion(bf16[2,1024,512]{1,2,0:T(8,128)(2,1)} %get-tuple-element.60, f32[1024,1536]{1,0:T(8,128)} %convert_element_type.165, f32[2,1024]{1,0:T(2,128)S(1)} %dynamic-slice_bitcast_fusion), kind=kOutput, calls=%fused_computation.3 | convolution fusion | flops 3227516928 | bytes 14688256 | tf_op jit(solution)/shard_map/etf,etd->efd/dot_general | solution.py:44
  189.6 3.4 convolution_bitcast_fusion.1
  194.7 3.4 convolution_bitcast_fusion
  203.4 8.9 %multiply_reduce_fusion.1 = bf16[1024,1536]{1,0:T(8,128)(2,1)} fusion(f32[2,1024]{1,0:T(2,128)S(1)} %dynamic-slice_bitcast_fusion, bf16[2,1024,512]{1,2,0:T(8,128)(2,1)} %get-tuple-element.60, bf16[2,512,1536]{2,1,0:T(8,128)(2,1)} %constant_dynamic-update-slice_fusion), kind=kOutput, calls=%fused_computation.2 | convolution fusion | flops 3232235520 | bytes 8396800 | tf_op jit(solution)/shard_map/etf,efd->etd/dot_general | solution.py:44
  212.5 40.9 %reduce-scatter.5.cloned.1.call-done = bf16[128,1536]{1,0:T(8,128)(2,1)} async-done(((bf16[1024,1536]{1,0:T(8,128)(2,1)}), bf16[128,1536]{1,0:T(8,128)(2,1)}) %reduce-scatter.5.cloned.1.call-update) | async-done | bytes 393232 | tf_op jit(solution)/shard_map/reduce_scatter | solution.py:120
  264.0 3.2 fusion.21
  286.5 88.5 %all-reduce.7.cloned.1.call-done = (bf16[2,1536,256]{1,2,0:T(8,128)(2,1)}, bf16[2,1536,256]{1,2,0:T(8,128)(2,1)}, bf16[2,256,1536]{2,1,0:T(8,128)(2,1)}) async-done(((bf16[2,1536,256]{1,2,0:T(8,128)(2,1)}, bf16[2,1536,256]{1,2,0:T(8,128)(2,1)}, bf16[2,256,1536]{2,1,0:T(8,128)(2,1)}), (bf16[2,1536,256]{1,2,0:T(8,128)(2,1)}, bf16[2,1536,256]{1,2,0:T(8,128)(2,1)}, ...) | async-done | bytes 4718608 | tf_op jit(solution)/shard_map/psum | solution.py:127
  375.0 3.1 copy.91
  378.1 3.1 copy.92
  381.1 3.6 convert_element_type.194
  387.4 41.0 %psum.56 = f32[2,1536]{1,0:T(2,128)} all-reduce(f32[2,1536]{1,0:T(2,128)} %pad_maximum_fusion.14), channel_id=1, replica_groups=mesh['dp'=2,'expert'=8,'tensor'=2] {'dp','expert','tensor'}, use_global_device_ids=true, to_apply=%region_13.14 | all-reduce | flops 3072 | bytes 24576 | tf_op jit(solution)/shard_map/psum | solution.py:169
  431.0 23.9 %reduce-scatter.3.cloned.1.call-done = bf16[128,1536]{1,0:T(8,128)(2,1)} async-done(((bf16[1024,1536]{1,0:T(8,128)(2,1)}), bf16[128,1536]{1,0:T(8,128)(2,1)}) %reduce-scatter.3.cloned.1.call-update) | async-done | bytes 393232 | tf_op jit(solution)/shard_map/reduce_scatter | solution.py:121
  454.9 3.3 subtract_add_fusion
  458.2 216.4 %all-reduce.5.cloned.1.call-done = (bf16[1536,768]{1,0:T(8,128)(2,1)}, bf16[1536,256]{1,0:T(8,128)(2,1)}, bf16[1536,256]{1,0:T(8,128)(2,1)}, bf16[768,1536]{1,0:T(8,128)(2,1)}) async-done(((bf16[1536,768]{1,0:T(8,128)(2,1)}, bf16[1536,256]{1,0:T(8,128)(2,1)}, bf16[1536,256]{1,0:T(8,128)(2,1)}, bf16[768,1536]{1,0:T(8,128)(2,1)}), (bf16[1536,768]{1,0:T(8,128)(2,1)}, bf16[1536,256]{1,0:T(8,128)(2,1)}, ...) | async-done | bytes 6291472 | tf_op jit(solution)/shard_map/psum | solution.py:168
  681.0 2.8 convert_element_type.185
  (239 shorter events, 80.7 us)
Async XLA Ops:
  7.2 13.7 %copy-start = (bf16[768,1536]{1,0:T(8,128)(2,1)S(1)}, bf16[768,1536]{1,0:T(8,128)(2,1)}, u32[]{:S(2)}) copy-start(bf16[768,1536]{1,0:T(8,128)(2,1)} %param.23) | copy-start | bytes 7077892
  7.2 67.1 %all-gather.5.cloned.1.call-start = ((), (), s32[]{:S(2)}) async-start(), calls=%async_computation.4 | async-start | bytes 3538944 | tf_op jit(solution)/shard_map/all_gather | solution.py:80
  8.0 128.2 %all-gather.3.cloned.1.call-start = ((), (), s32[]{:S(2)}) async-start(), calls=%async_computation.2 | async-start | bytes 3538944 | tf_op jit(solution)/shard_map/all_gather | solution.py:104
  8.0 3.7 collective-permute-start
  10.9 9.1 %copy-start.41 = (pred[256,256]{0,1:T(8,128)(4,1)}, pred[256,256]{0,1:T(8,128)(4,1)S(1)}, u32[]{:S(2)}) copy-start(pred[256,256]{0,1:T(8,128)(4,1)S(1)} %compare_and_fusion) | copy-start | bytes 196612
  11.7 10.1 %copy-start.15 = (bf16[128,1536]{1,0:T(8,128)(2,1)}, bf16[128,1536]{1,0:T(8,128)(2,1)S(1)}, u32[]{:S(2)}) copy-start(bf16[128,1536]{1,0:T(8,128)(2,1)S(1)} %collective-permute-done) | copy-start | bytes 1179652
  21.8 2.4 collective-permute-start.1
  26.4 227.1 %reduce-scatter.5.cloned.1.call-start = ((), (), s32[]{:S(2)}) async-start(), calls=%async_computation.5 | async-start | bytes 3538944 | tf_op jit(solution)/shard_map/reduce_scatter | solution.py:120
  26.4 40.8 %collective-permute-start.4 = (bf16[2,256,1536]{2,1,0:T(8,128)(2,1)}, bf16[2,256,1536]{2,1,0:T(8,128)(2,1)}, u32[]{:S(2)}, u32[]{:S(2)}) collective-permute-start(bf16[2,256,1536]{2,1,0:T(8,128)(2,1)} %param.26), channel_id=1, source_target_pairs={{0,1},{1,0},{2,3},{3,2},{4,5},{5,4},{6,7},{7,6},{8,9},{9,8},{10,11... | collective-permute-start | bytes 4718600 | tf_op jit(solution)/shard_map/ppermute | solution.py:16
  29.2 50.5 %collective-permute-start.3 = (bf16[2,1536,256]{1,2,0:T(8,128)(2,1)}, bf16[2,1536,256]{1,2,0:T(8,128)(2,1)}, u32[]{:S(2)}, u32[]{:S(2)}) collective-permute-start(bf16[2,1536,256]{1,2,0:T(8,128)(2,1)} %copy.79), channel_id=1, source_target_pairs={{0,1},{1,0},{2,3},{3,2},{4,5},{5,4},{6,7},{7,6},{8,9},{9,8},{10,11... | collective-permute-start | bytes 4718600 | tf_op jit(solution)/shard_map/ppermute | solution.py:16
  32.2 110.3 %collective-permute-start.2 = (bf16[2,1536,256]{1,2,0:T(8,128)(2,1)}, bf16[2,1536,256]{1,2,0:T(8,128)(2,1)}, u32[]{:S(2)}, u32[]{:S(2)}) collective-permute-start(bf16[2,1536,256]{1,2,0:T(8,128)(2,1)} %copy.77), channel_id=1, source_target_pairs={{0,1},{1,0},{2,3},{3,2},{4,5},{5,4},{6,7},{7,6},{8,9},{9,8},{10,11... | collective-permute-start | bytes 4718600 | tf_op jit(solution)/shard_map/ppermute | solution.py:16
  136.1 13.0 %slice-start = ((s8[6291456]{0:T(1024)(128)(4,1)}), s8[4194304]{0:T(1024)(128)(4,1)S(1)}, s32[]{:S(2)}) async-start(s8[6291456]{0:T(1024)(128)(4,1)} %bitcast.159), calls=%async_computation.8 | async-start | bytes 8388608
  149.1 9.5 %copy-start.11 = (bf16[2,1536,256]{1,2,0:T(8,128)(2,1)S(1)}, bf16[2,1536,256]{1,2,0:T(8,128)(2,1)}, u32[]{:S(2)}) copy-start(bf16[2,1536,256]{1,2,0:T(8,128)(2,1)} %copy.79) | copy-start | bytes 4718596
  180.2 194.8 %all-reduce.7.cloned.1.call-start = ((), (), s32[]{:S(2)}) async-start(), calls=%async_computation.7 | async-start | bytes 9437184 | tf_op jit(solution)/shard_map/psum | solution.py:127
  188.0 10.4 %collective-permute-start.9 = (bf16[2,256,1536]{2,1,0:T(8,128)(2,1)S(1)}, bf16[2,256,1536]{2,1,0:T(8,128)(2,1)S(1)}, u32[]{:S(2)}, u32[]{:S(2)}) collective-permute-start(bf16[2,256,1536]{2,1,0:T(8,128)(2,1)S(1)} %split.101), channel_id=1, source_target_pairs={{0,1},{1,0},{2,3},{3,2},{4,5},{5,4},{6,7},{7,6},{8,9},{9,8},{10,11... | collective-permute-start | bytes 4718600 | tf_op jit(solution)/shard_map/ppermute | solution.py:16
  193.3 6.7 collective-permute-start.7
  198.3 3.5 collective-permute-start.8
  203.4 251.6 %reduce-scatter.3.cloned.1.call-start = ((), (), s32[]{:S(2)}) async-start(), calls=%async_computation.3 | async-start | bytes 3538944 | tf_op jit(solution)/shard_map/reduce_scatter | solution.py:121
  212.3 41.2 %copy-start.52 = (f32[128]{0:T(128)S(1)}, f32[128]{0:T(128)}, u32[]{:S(2)}) copy-start(f32[128]{0:T(128)} %copy-done.51) | copy-start | bytes 1540
  212.3 43.0 %copy-start.56 = (f32[128]{0:T(128)S(1)}, f32[128]{0:T(128)}, u32[]{:S(2)}) copy-start(f32[128]{0:T(128)} %get-tuple-element.79) | copy-start | bytes 1540
  212.3 462.3 %all-reduce.5.cloned.1.call-start = ((), (), s32[]{:S(2)}) async-start(), calls=%async_computation.6 | async-start | bytes 12582912 | tf_op jit(solution)/shard_map/psum | solution.py:168
  256.7 1.8 collective-permute-start.5
  285.1 99.7 %collective-permute-start.6 = (f32[128,1536]{1,0:T(8,128)}, f32[128,1536]{1,0:T(8,128)}, u32[]{:S(2)}, u32[]{:S(2)}) collective-permute-start(f32[128,1536]{1,0:T(8,128)} %slice.53), channel_id=1, source_target_pairs={{0,1},{1,0},{2,3},{3,2},{4,5},{5,4},{6,7},{7,6},{8,9},{9,8},{10,11... | collective-permute-start | bytes 2359304 | tf_op jit(solution)/shard_map/ppermute | solution.py:16
  384.8 70.2 %copy-start.5 = (bf16[128,1536]{1,0:T(8,128)(2,1)S(1)}, bf16[128,1536]{1,0:T(8,128)(2,1)}, u32[]{:S(2)}) copy-start(bf16[128,1536]{1,0:T(8,128)(2,1)} %param.27) | copy-start | bytes 1179652
  (61 other events, 179.2 us)
Sparse Core Ops, SparseCore 0:
  10.2 64.0 all-gather.4
  77.1 58.9 all-gather.2
  180.3 73.0 reduce-scatter.4
  255.9 119.0 all-reduce.6
  379.4 75.4 reduce-scatter.2
  462.9 211.6 all-reduce.4

commit v2 on v1

v2 whole, which is shorter than its diff:
```python
import functools

import jax
import jax.numpy as jnp
import numpy as np
from jax import lax
from jax.experimental import pallas as pl
from jax.experimental.pallas import tpu as pltpu
from jax.sharding import PartitionSpec as P

HEAD_DIM = 64
EPS = 1e-05
ATTN_SCALE = 0.015625
THETA = 10000.0
NEG_FILL = -1e30
F32 = jnp.float32
BF16 = jnp.bfloat16
NO_COST = pl.CostEstimate(flops=1, bytes_accessed=1, transcendentals=0)


def after(values, token):
    return lax.optimization_barrier((values, token))[0]


def swap(values):
    return lax.ppermute(values, "tensor", [(0, 1), (1, 0)])


def shift_dp(values, step):
    count = lax.axis_size("dp")
    return lax.ppermute(values, "dp", [(i, (i + step) % count) for i in range(count)])


def grid_sizes():
    count = lax.axis_size("expert")
    outer = 4 if count % 4 == 0 else count
    return outer, count // outer


def shift_outer(values):
    outer, inner = grid_sizes()
    pairs = [(((o + 1) % outer) * inner + i, o * inner + i) for o in range(outer) for i in range(inner)]
    return lax.ppermute(values, "expert", pairs)


def shift_inner(values):
    outer, inner = grid_sizes()
    pairs = [(o * inner + (i + 1) % inner, o * inner + i) for o in range(outer) for i in range(inner)]
    return lax.ppermute(values, "expert", pairs)


def inner_line(block):
    line = [block]
    for _ in range(1, grid_sizes()[1]):
        line.append(shift_inner(line[-1]))
    return line


def inner_sum(parts):
    inner, total = len(parts), parts[1 % len(parts)]
    for j in range(2, inner + 1):
        total = shift_inner(total.astype(BF16)).astype(F32) + parts[j % inner].astype(F32)
    return total


def together(*values):
    return lax.optimization_barrier(values)


def sum_all(values):
    for axis in ("tensor", "expert", "dp"):
        count, bit = lax.axis_size(axis), 1
        while bit < count:
            values = values + lax.ppermute(values, axis, [(i, i ^ bit) for i in range(count)])
            bit *= 2
    return values


def norm_forward(values, gain_vector):
    inv_scale = lax.rsqrt(jnp.mean(values * values, axis=-1, keepdims=True) + EPS)
    return (values * inv_scale * gain_vector, inv_scale)


def norm_backward(values, inv_scale, gain_vector, upstream):
    weighted = upstream * gain_vector
    inner = jnp.mean(weighted * values, axis=-1, keepdims=True)
    value_gradient = inv_scale * weighted - values * (inv_scale * inv_scale * inv_scale) * inner
    grad_gain = jnp.sum(upstream * values * inv_scale, axis=0)
    return (value_gradient, grad_gain)


def dot(spec, left, right, kind=F32):
    return jnp.einsum(spec, left, right, preferred_element_type=kind)

def dot_t(left, right):
    return lax.dot_general(left, right, (((1,), (1,)), ((), ())), preferred_element_type=F32)


def full_spec(*shape):
    return pl.BlockSpec(shape, lambda *_: (0,) * len(shape))


def rope_tables(length, width):
    half = HEAD_DIM // 2
    frequency = (THETA ** (-np.arange(half, dtype=np.float32) * 2.0 / HEAD_DIM)).astype(np.float32)
    angle = np.arange(length, dtype=np.float32)[:, None] * frequency[None, :]
    cosine, sine = np.cos(angle.astype(np.float64)), np.sin(angle.astype(np.float64))
    cosine = np.concatenate([cosine, cosine], axis=1)
    sine = np.concatenate([-sine, sine], axis=1)
    copies = width // HEAD_DIM
    return np.tile(cosine, (1, copies)).astype(np.float32), np.tile(sine, (1, copies)).astype(np.float32)


def turn(values, cosine, sine):
    width, half = values.shape[1], HEAD_DIM // 2
    copies = width // cosine.shape[1]
    lane = lax.broadcasted_iota(jnp.int32, values.shape, 1)
    first = lax.rem(lane, HEAD_DIM) < half
    other = jnp.where(first, pltpu.roll(values, width - half, 1), pltpu.roll(values, half, 1))
    return values * jnp.concatenate([cosine] * copies, 1) + other * jnp.concatenate([sine] * copies, 1)


def masked_scores(query, key, allowed):
    return jnp.where(allowed, dot_t(query, key) * ATTN_SCALE, NEG_FILL)


def allowed_pairs(segs):
    length = segs.shape[1]
    row = lax.broadcasted_iota(jnp.int32, (length, length), 0)
    column = lax.broadcasted_iota(jnp.int32, (length, length), 1)
    seg_row = segs.astype(F32)
    seg_column = jnp.sum(jnp.where(row == column, seg_row, 0.0), axis=1, keepdims=True)
    return (column <= row) & (seg_row == seg_column)


def row_places(meta, rows):
    own = pl.ds(pl.multiple_of(meta[0] * rows, rows), rows)
    other = pl.ds(pl.multiple_of((1 - meta[0]) * rows, rows), rows)
    return own, other


def attend_kernel(
    meta, own_ref, other_ref, gain_ref, segs, cos_ref, sin_ref, wq, wk, wv, wo,
    hidden_out, q_out, k_out, v_out, mixed_out, log_out, own_out, other_out, x_s, part_s,
):
    rows = own_ref.shape[0]
    own, other = row_places(meta, rows)
    x_s[own, :] = own_ref[...].astype(F32)
    x_s[other, :] = other_ref[...].astype(F32)
    x = x_s[...]
    scale = lax.rsqrt(jnp.mean(x * x, axis=-1, keepdims=True) + EPS)
    hidden = (x * scale * gain_ref[...]).astype(BF16)
    hidden_out[...] = hidden
    cosine, sine = cos_ref[...], sin_ref[...]
    q_out[...] = turn(jnp.dot(hidden, wq[...], preferred_element_type=F32), cosine, sine).astype(BF16)
    k_out[...] = turn(jnp.dot(hidden, wk[...], preferred_element_type=F32), cosine, sine).astype(BF16)
    v_out[...] = jnp.dot(hidden, wv[...], preferred_element_type=F32).astype(BF16)
    allowed = allowed_pairs(segs[...])
    heads, heads_kv = wq.shape[1] // HEAD_DIM, wk.shape[1] // HEAD_DIM
    group = heads // heads_kv
    for g in range(heads_kv):
        key = k_out[:, g * HEAD_DIM : (g + 1) * HEAD_DIM]
        value = v_out[:, g * HEAD_DIM : (g + 1) * HEAD_DIM]
        for h in range(g * group, (g + 1) * group):
            at = slice(h * HEAD_DIM, (h + 1) * HEAD_DIM)
            scores = masked_scores(q_out[:, at], key, allowed)
            top = jnp.max(scores, axis=-1, keepdims=True)
            log_total = top + jnp.log(jnp.sum(jnp.exp(scores - top), axis=-1, keepdims=True))
            log_out[:, h : h + 1] = log_total
            prob = jnp.exp(scores - log_total).astype(BF16)
            mixed_out[:, at] = jnp.dot(prob, value, preferred_element_type=F32).astype(BF16)
    part_s[...] = jnp.dot(mixed_out[...], wo[...], preferred_element_type=F32)
    own_out[...] = part_s[own, :]
    other_out[...] = part_s[other, :]


def attend(meta, own, other, gain, segs, wq, wk, wv, wo):
    rows, width = own.shape
    length = segs.shape[1]
    cosine, sine = rope_tables(length, 128)
    operands = (own, other, gain[None, :], segs, cosine, sine, wq, wk, wv, wo)
    shapes = [
        ((length, width), BF16),
        ((length, wq.shape[1]), BF16),
        ((length, wk.shape[1]), BF16),
        ((length, wv.shape[1]), BF16),
        ((length, wq.shape[1]), BF16),
        ((length, 128), F32),
        ((rows, width), F32),
        ((rows, width), F32),
    ]
    return pl.pallas_call(
        attend_kernel,
        out_shape=[jax.ShapeDtypeStruct(*shape) for shape in shapes],
        grid_spec=pltpu.PrefetchScalarGridSpec(
            num_scalar_prefetch=1,
            grid=(1,),
            in_specs=[full_spec(*t.shape) for t in operands],
            out_specs=[full_spec(*shape) for shape, _ in shapes],
            scratch_shapes=[pltpu.VMEM((length, width), F32)] * 2,
        ),
        compiler_params=pltpu.CompilerParams(vmem_limit_bytes=56 * 1024 * 1024),
        cost_estimate=NO_COST,
    )(meta, *operands)


def attend_back_kernel(
    shares, meta, b_ref, segs, cos_ref, sin_ref, wq, wk, wv, wo,
    q_ref, k_ref, v_ref, mixed_ref, log_ref, *refs,
):
    share_outs, (own_out, other_out, grad_s, dq_s, part_s) = refs[:shares], refs[shares:]
    own, other = row_places(meta, own_out.shape[0])
    grad_s[...] = dot_t(b_ref[...], wo[...]).astype(BF16)
    cosine, sine = cos_ref[...], -sin_ref[...]
    allowed = allowed_pairs(segs[...])
    wide, narrow = wq.shape[1], wk.shape[1]
    heads, heads_kv = wide // HEAD_DIM, narrow // HEAD_DIM
    group = heads // heads_kv

    def transposed_dot(left, right):
        return lax.dot_general(left, right, (((0,), (0,)), ((), ())), preferred_element_type=F32)

    for g in range(heads_kv):
        there = slice(g * HEAD_DIM, (g + 1) * HEAD_DIM)
        key, value = k_ref[:, there], v_ref[:, there]
        grad_key = grad_value = 0.0
        for h in range(g * group, (g + 1) * group):
            at = slice(h * HEAD_DIM, (h + 1) * HEAD_DIM)
            query, grad = q_ref[:, at], grad_s[:, at]
            prob = jnp.exp(masked_scores(query, key, allowed) - log_ref[:, h : h + 1])
            delta = jnp.sum(grad.astype(F32) * mixed_ref[:, at].astype(F32), axis=-1, keepdims=True)
            grad_scores = (prob * (dot_t(grad, value) - delta) * ATTN_SCALE).astype(BF16)
            dq_s[:, at] = jnp.dot(grad_scores, key, preferred_element_type=F32)
            grad_key = grad_key + transposed_dot(grad_scores, query)
            grad_value = grad_value + transposed_dot(prob.astype(BF16), grad)
        dq_s[:, wide + g * HEAD_DIM : wide + (g + 1) * HEAD_DIM] = grad_key
        at = wide + narrow + g * HEAD_DIM
        dq_s[:, at : at + HEAD_DIM] = grad_value
    dq = turn(dq_s[:, :wide], cosine, sine).astype(BF16)
    dk = turn(dq_s[:, wide : wide + narrow], cosine, sine).astype(BF16)
    dv = dq_s[:, wide + narrow :].astype(BF16)
    part_s[...] = dot_t(dq, wq[...]) + dot_t(dk, wk[...]) + dot_t(dv, wv[...])
    own_out[...] = part_s[own, :]
    other_out[...] = part_s[other, :]
    for r in range(shares):

        @pl.when(meta[1] == r)
        def _():
            for step in range(shares):
                at = 0
                for part in (dq, dk, dv):
                    size = part.shape[1] // shares
                    index = (r + step) % shares
                    share_outs[step][:, at : at + size] = part[:, index * size : (index + 1) * size]
                    at += size


def attend_back(meta, shares, resid, segs, wq, wk, wv, wo, q, k, v, mixed, log_total):
    length, width = resid.shape
    cosine, sine = rope_tables(length, 128)
    operands = (resid, segs, cosine, sine, wq, wk, wv, wo, q, k, v, mixed, log_total)
    columns = wq.shape[1] + wk.shape[1] + wv.shape[1]
    shapes = [((length, columns // shares), BF16)] * shares
    shapes += [((length // 2, width), F32)] * 2
    return pl.pallas_call(
        functools.partial(attend_back_kernel, shares),
        out_shape=[jax.ShapeDtypeStruct(*shape) for shape in shapes],
        grid_spec=pltpu.PrefetchScalarGridSpec(
            num_scalar_prefetch=1,
            grid=(1,),
            in_specs=[full_spec(*t.shape) for t in operands],
            out_specs=[full_spec(*shape) for shape, _ in shapes],
            scratch_shapes=[
                pltpu.VMEM((length, wq.shape[1]), BF16),
                pltpu.VMEM((length, columns), F32),
                pltpu.VMEM((length, width), F32),
            ],
        ),
        compiler_params=pltpu.CompilerParams(vmem_limit_bytes=56 * 1024 * 1024),
        cost_estimate=NO_COST,
    )(meta, *operands)


def expert_kernel(inner, aliased, experts, meta, *refs):
    blocks, payloads, refs = refs[:inner], refs[inner : 2 * inner], refs[2 * inner :]
    weight_refs, refs = refs[:6], refs[6 + aliased :]
    tokens_out, upstream_out, mix_out = refs[:3]
    used_out, gate_out, up_out = refs[3:5], refs[5:7], refs[7:9]
    in_out = refs[9 : 9 + inner]
    table, mix_total, in_total = refs[9 + inner :]
    rows, width = blocks[0].shape
    expert = pl.program_id(0)

    def place(j):
        return pl.ds(pl.multiple_of(lax.rem(meta[1] + j, inner) * rows, rows), rows)

    @pl.when(expert == 0)
    def _():
        for j in range(inner):
            tokens_out[place(j), :] = blocks[j][...]
            upstream_out[place(j), :] = payloads[j][:, :width]
            table[place(j), :] = payloads[j][:, width:].astype(F32)
        mix_total[...] = jnp.zeros_like(mix_total)
        in_total[...] = jnp.zeros_like(in_total)

    lane = lax.broadcasted_iota(jnp.int32, table.shape, 1)
    wanted = (lax.rem(lane, experts) == meta[2] + expert) & (lane < 3 * experts)
    weight = jnp.sum(jnp.where(wanted, table[...], 0.0), axis=1, keepdims=True)
    for half in range(2):
        gate, up, down = (weight_refs[2 * i + half][0] for i in range(3))
        pre_gate = jnp.dot(tokens_out[...], gate, preferred_element_type=F32)
        pre_up = jnp.dot(tokens_out[...], up, preferred_element_type=F32)
        grad_act = dot_t(upstream_out[...], down) * weight
        gate_sigmoid = 1.0 / (1.0 + jnp.exp(-pre_gate))
        silu = pre_gate * gate_sigmoid
        used = (silu * pre_up * weight).astype(BF16)
        grad_gate = grad_act * pre_up * gate_sigmoid * (1.0 + pre_gate * (1.0 - gate_sigmoid))
        grad_up = grad_act * silu
        used_out[half][0] = used
        gate_out[half][0] = grad_gate.astype(BF16)
        up_out[half][0] = grad_up.astype(BF16)
        mix_total[...] += jnp.dot(used, down, preferred_element_type=F32)
        in_total[...] += dot_t((grad_gate * weight).astype(BF16), gate) + dot_t(
            (grad_up * weight).astype(BF16), up
        )

    @pl.when(expert == pl.num_programs(0) - 1)
    def _():
        mix_out[...] = mix_total[...].astype(BF16)
        for j in range(inner):
            in_out[j][...] = in_total[place(j), :].astype(BF16)


def run_experts(meta, blocks, payloads, expert_weights, buffers, total, expert_count):
    inner = len(blocks)
    rows, width = blocks[0].shape
    experts, half = expert_weights[0].shape[0], expert_weights[0].shape[2]
    chunk = inner * rows
    extra = payloads[0].shape[1] - width
    by_chunk = pl.BlockSpec((chunk, width), lambda e, m: (m[0], 0))
    per_expert = pl.BlockSpec((1, chunk, half), lambda e, m: (e, m[0], 0))
    spread = pl.BlockSpec((1, width, half), lambda e, m: (e, 0, 0))
    tall = pl.BlockSpec((1, half, width), lambda e, m: (e, 0, 0))
    shapes = [jax.ShapeDtypeStruct((total, width), BF16)] * 3
    shapes += [jax.ShapeDtypeStruct((experts, total, half), BF16)] * 6
    first = 1 + 2 * inner + 6
    return pl.pallas_call(
        functools.partial(expert_kernel, inner, len(buffers), expert_count),
        out_shape=shapes + [jax.ShapeDtypeStruct((rows, width), BF16)] * inner,
        grid_spec=pltpu.PrefetchScalarGridSpec(
            num_scalar_prefetch=1,
            grid=(experts,),
            in_specs=[full_spec(rows, width)] * inner
            + [full_spec(rows, width + extra)] * inner
            + [spread] * 4
            + [tall] * 2
            + [pl.BlockSpec(memory_space=pl.ANY)] * len(buffers),
            out_specs=[by_chunk] * 3 + [per_expert] * 6 + [full_spec(rows, width)] * inner,
            scratch_shapes=[
                pltpu.VMEM((chunk, extra), F32),
                pltpu.VMEM((chunk, width), F32),
                pltpu.VMEM((chunk, width), F32),
            ],
        ),
        input_output_aliases={first + i: i for i in range(len(buffers))},
        compiler_params=pltpu.CompilerParams(vmem_limit_bytes=56 * 1024 * 1024),
        cost_estimate=NO_COST,
    )(meta, *blocks, *payloads, *expert_weights, *buffers)


def place_kernel(sizes, aliased, meta, block_ref, *refs):
    at = 0
    for size, out in zip(sizes, refs[aliased:]):
        out[...] = block_ref[0, :, at : at + size].astype(F32)
        at += size


def place_line(meta, pieces, sizes, shapes, buffers):
    count, rows, width = pieces.shape
    low = [pl.BlockSpec((rows, size), lambda i, m: (m[4 * i], m[4 * i + 1])) for size in sizes[:-1]]
    low.append(pl.BlockSpec((rows, sizes[-1]), lambda i, m: (m[4 * i + 2], m[4 * i + 3])))
    return pl.pallas_call(
        functools.partial(place_kernel, sizes, len(buffers)),
        out_shape=[jax.ShapeDtypeStruct(shape, F32) for shape in shapes],
        grid_spec=pltpu.PrefetchScalarGridSpec(
            num_scalar_prefetch=1,
            grid=(count,),
            in_specs=[pl.BlockSpec((1, rows, width), lambda i, m: (i, 0, 0))]
            + [pl.BlockSpec(memory_space=pl.ANY)] * len(buffers),
            out_specs=low,
        ),
        input_output_aliases={2 + i: i for i in range(len(buffers))},
        cost_estimate=NO_COST,
    )(meta, pieces, *buffers)


def body(
    activations,
    segments,
    routes,
    route_weights,
    norm_attn_gain,
    norm_ffn_gain,
    query_weight,
    key_matrix,
    value_matrix,
    output_projection_weight,
    expert_gate,
    expert_up,
    expert_down,
    grad_output,
):
    tensor_rank = lax.axis_index("tensor")
    dp_rank = lax.axis_index("dp")
    dp_count = lax.axis_size("dp")
    outer, inner = grid_sizes()
    outer_rank = lax.axis_index("expert") // inner
    inner_rank = lax.axis_index("expert") % inner
    rows, width = activations.shape
    experts_here = expert_gate.shape[0]
    expert_count = experts_here * lax.axis_size("expert")

    named = routes[:, :, None] == jnp.arange(expert_count, dtype=jnp.int32)
    weight_table = jnp.sum(jnp.where(named, route_weights[:, :, None], 0.0), axis=1)
    high = lax.reduce_precision(weight_table, 8, 7)
    middle = lax.reduce_precision(weight_table - high, 8, 7)
    low = weight_table - high - middle
    table = jnp.concatenate([high, middle, low], axis=1).astype(BF16)
    table = jnp.pad(table, ((0, 0), (0, -table.shape[1] % 128)))
    payload = jnp.concatenate([grad_output, table], axis=1)
    up_line, up_next = together(inner_line(payload), shift_outer(payload))
    heads_meta = jnp.stack([tensor_rank, dp_rank]).astype(jnp.int32)
    attn_weights = (query_weight, key_matrix, value_matrix, output_projection_weight)
    hidden, q, k, v, mixed, log_total, attn_own, attn_other = attend(
        heads_meta, activations, swap(activations), norm_attn_gain, segments, *attn_weights
    )
    x_own = activations.astype(F32)
    attn_own, attn_other, up_line, up_next = together(attn_own, attn_other, up_line, up_next)
    residual = x_own + attn_own + swap(attn_other)
    normed_two, scale_two = norm_forward(residual, norm_ffn_gain)

    expert_weights = []
    for weights_own in (expert_gate, expert_up, expert_down):
        expert_weights += [weights_own, swap(weights_own)]
    first_expert = lax.axis_index("expert") * experts_here

    upstream, tokens = {0: up_line}, {}
    next_up, next_tokens = up_next, normed_two.astype(BF16)
    buffers, in_parts, lines, running = [], {}, {}, None
    peers = halves = None
    for turn_index in range(1, outer + 4):
        step = {}
        if turn_index < outer:
            step["up_line"] = inner_line(next_up)
            if turn_index + 1 < outer:
                step["up_next"] = shift_outer(next_up)
        if turn_index - 1 < outer:
            step["line"] = inner_line(next_tokens)
            if turn_index < outer:
                step["next"] = shift_outer(next_tokens)
        summed = [turn_index - 3] if 1 <= turn_index - 3 < outer else []
        summed += [0] if turn_index == outer + 1 else []
        if summed:
            step["sums"] = {i: inner_sum(in_parts[i]) for i in summed}
        at = turn_index - 4
        if 1 <= at < outer:
            held = lines[at] if running is None else running.astype(F32) + lines[at].astype(F32)
            step["running"] = shift_outer(held.astype(BF16))
        chunk = turn_index - 2
        if 0 <= chunk < outer:
            meta = [(outer_rank + chunk) % outer, inner_rank, first_expert]
            step["made"] = run_experts(
                jnp.stack(meta).astype(jnp.int32), tokens[chunk], upstream[chunk],
                expert_weights, buffers, outer * inner * rows, expert_count,
            )
        if chunk == outer:
            tokens_all, upstream_all, mix_all, *pairs = buffers
            jobs = [
                ("etf,td->edf", pairs[2:4], tokens_all),
                ("etf,td->edf", pairs[4:6], tokens_all),
                ("etf,td->efd", pairs[0:2], upstream_all),
            ]
            step["peers"] = [dot(spec, pair[1], side, BF16) for spec, pair, side in jobs]
        if chunk == outer + 1:
            step["halves"] = [
                (dot(spec, pair[0], side) + swap(other).astype(F32)).astype(BF16)
                for (spec, pair, side), other in zip(jobs, peers)
            ]
        (step,) = together(step)
        if "up_line" in step:
            upstream[turn_index] = step["up_line"]
        next_up = step.get("up_next")
        if "line" in step:
            tokens[turn_index - 1] = step["line"]
        next_tokens = step.get("next")
        lines.update(step.get("sums", {}))
        running = step.get("running", running)
        if "made" in step:
            buffers, in_parts[chunk] = list(step["made"][:9]), step["made"][9:]
        peers = step.get("peers", peers)
        halves = step.get("halves", halves)
    grad_h_own = running.astype(F32) + lines[0].astype(F32)

    def sum_dp(half):
        bit, found = 1, []
        while bit < dp_count:
            found.append(lax.ppermute(half, "dp", [(i, i ^ bit) for i in range(dp_count)]))
            bit *= 2
            if bit < dp_count:
                half = (half.astype(F32) + found.pop().astype(F32)).astype(BF16)
        return half, *found

    def total(pair):
        return sum(t.astype(F32) for t in pair)

    grad_norm_part, grad_ffn_gain = norm_backward(residual, scale_two, norm_ffn_gain, grad_h_own)
    grad_resid = grad_output.astype(F32) + grad_norm_part
    resid_own = grad_resid.astype(BF16)
    resid_other = swap(resid_own)
    resid_full = jnp.where(
        tensor_rank == 0,
        jnp.concatenate([resid_own, resid_other], axis=0),
        jnp.concatenate([resid_other, resid_own], axis=0),
    )
    expert_mix = lax.psum_scatter(
        after(mix_all, resid_full), "expert", scatter_dimension=0, tiled=True
    )
    *shares, dh_own, dh_other = attend_back(
        heads_meta, dp_count, resid_full, segments, *attn_weights, q, k, v, mixed, log_total,
    )

    hidden_all, mixed_all = [hidden], [mixed]
    for step in range(1, dp_count):
        other = shift_dp(activations, step)
        other = jnp.concatenate([other, swap(other)], axis=0)
        other = jnp.where(tensor_rank == 0, other, jnp.roll(other, rows, 0)).astype(F32)
        hidden_all.append(norm_forward(other, norm_attn_gain)[0].astype(BF16))
        mixed_all.append(shift_dp(mixed, step))
    length, share_width = resid_full.shape[0], width // dp_count

    def columns(index):
        return lax.dynamic_slice_in_dim(resid_full, index * share_width, share_width, 1)

    resid_shares = [columns(dp_rank)]
    for step in range(1, dp_count):
        resid_shares.append(shift_dp(columns((dp_rank + step) % dp_count), step))
    shares, resid_shares = together(shares, resid_shares)
    all_shares = [shares[0]] + [shift_dp(shares[step], step) for step in range(1, dp_count)]
    gate_pair = sum_dp(after(halves[0], all_shares))
    qkv_part = dot("sd,sa->da", jnp.concatenate(hidden_all, 0), jnp.concatenate(all_shares, 0), BF16)
    parts = width // mixed.shape[1]
    mix_part = dot(
        "sa,shb->hab",
        jnp.concatenate(mixed_all, 0),
        jnp.concatenate(resid_shares, 0).reshape(length * dp_count, parts, share_width // parts),
        BF16,
    )
    dense_part = jnp.concatenate([qkv_part, mix_part.reshape(width, -1)], axis=1)
    block = width // (outer * inner)

    def row_terms(part, step):
        start = (outer_rank + step) % outer * inner
        return [
            lax.dynamic_slice_in_dim(part, (start + (inner_rank + j) % inner) * block, block, 0)
            for j in range(inner)
        ]

    held, running = {}, None
    for turn_index in range(outer):
        step = {"line": inner_sum(row_terms(dense_part, (turn_index + 1) % outer))}
        if turn_index:
            value = held[turn_index]
            value = value if running is None else running.astype(F32) + value.astype(F32)
            step["running"] = shift_outer(value.astype(BF16))
        if turn_index == outer - 1:
            step["gate"] = gate_pair
        step, dense_part = together(step, dense_part)
        held[(turn_index + 1) % outer] = step["line"]
        running = step.get("running")
        gate_pair = step.get("gate", gate_pair)
    reduced = (running.astype(F32) + held[0].astype(F32)).astype(BF16)
    sizes = [t.shape[1] // dp_count for t in (query_weight, key_matrix, value_matrix)]
    sizes.append(share_width // parts)
    shapes = [t.shape for t in (query_weight, key_matrix, value_matrix)] + [(width // parts, width)]
    expert_mix, residual = after((expert_mix, residual), reduced)
    block_out = (residual + expert_mix.astype(F32)).astype(BF16)
    grad_h_one = dh_own + swap(dh_other)
    scale_one = lax.rsqrt(jnp.mean(x_own * x_own, axis=-1, keepdims=True) + EPS)
    grad_x_part, grad_attn_gain = norm_backward(x_own, scale_one, norm_attn_gain, grad_h_one)
    grad_input = grad_resid + grad_x_part
    gains = sum_all(jnp.stack([grad_attn_gain, grad_ffn_gain]))
    if all(size % 128 == 0 for size in sizes):
        pieces = [reduced] + [shift_dp(reduced, step) for step in range(1, dp_count)]
        (pieces,) = together(pieces)
        up_pair = sum_dp(after(halves[1], pieces))
        dense, turn_next, lines = [], jnp.stack(pieces), {}
        for turn_index in range(outer + 1):
            step = {"line": inner_line(turn_next)} if turn_next is not None else {}
            if turn_index + 1 < outer:
                step["next"] = shift_outer(turn_next)
            if turn_index:
                made = dense
                for j in range(inner):
                    index = (outer_rank + turn_index - 1) % outer * inner + (inner_rank + j) % inner
                    meta = []
                    for turn in range(dp_count):
                        share = (dp_rank - turn) % dp_count
                        per = outer * inner // parts
                        meta += [index, share, index % per, share * parts + index // per]
                    made = place_line(
                        jnp.stack(meta).astype(jnp.int32), lines[turn_index - 1][j], sizes, shapes, made
                    )
                step["made"] = made
            if turn_index == 2:
                step["up"] = up_pair
            if turn_index == outer:
                step["finished"] = (block_out, grad_input, gains)
            (step,) = together(step)
            if turn_index == 2:
                up_pair = step["up"]
                down_pair = sum_dp(after(halves[2], up_pair))
            lines[turn_index] = step.get("line")
            turn_next, dense = step.get("next"), step.get("made", [])
            block_out, grad_input, gains = step.get("finished", (block_out, grad_input, gains))
        gate_sum, up_sum = total(gate_pair), total(up_pair)
        down_sum = total(down_pair)
    else:
        up_pair, down_pair = (sum_dp(half) for half in halves[1:])
        gate_sum, up_sum, down_sum = (total(pair) for pair in (gate_pair, up_pair, down_pair))
        gathered = lax.all_gather(reduced, ("dp", "expert"), axis=0, tiled=True)
        gathered = gathered.reshape(dp_count, width, -1).astype(F32)
        starts = [sum(sizes[:i]) for i in range(len(sizes))]
        dense = [gathered[:, :, at : at + size] for at, size in zip(starts, sizes)]
        dense[:-1] = [t.transpose(1, 0, 2).reshape(width, -1) for t in dense[:-1]]
        mix_w = dense[-1].reshape(dp_count, parts, width // parts, -1)
        dense[-1] = mix_w.transpose(2, 0, 1, 3).reshape(width // parts, width)
    return (
        block_out,
        grad_input,
        gains[0],
        gains[1],
        *dense,
        gate_sum,
        up_sum,
        down_sum,
    )


def solution(mesh):
    tokens = P(("dp", "expert", "tensor"), None)
    whole = P()
    columns = P(None, "tensor")
    hidden_last = P("expert", None, "tensor")
    hidden_mid = P("expert", "tensor", None)
    mixer = P("tensor", None)
    return jax.shard_map(
        body,
        mesh=mesh,
        in_specs=(
            tokens,
            P(("dp", "expert"), None),
            tokens,
            tokens,
            whole,
            whole,
            columns,
            columns,
            columns,
            mixer,
            hidden_last,
            hidden_last,
            hidden_mid,
            tokens,
        ),
        out_specs=(
            tokens,
            tokens,
            whole,
            whole,
            columns,
            columns,
            columns,
            mixer,
            hidden_last,
            hidden_last,
            hidden_mid,
        ),
        check_vma=False,
    )
```

time: 698 us -> 419 us (0.60)
  waiting for transfers between devices: 435 us -> 135 us
  Pallas kernels: 0 us -> 96.1 us
  starting transfers between devices: 2.72 us -> 83.2 us
  blocking collectives: 73.3 us -> 0 us
  matrix products: 89.9 us -> 20.7 us
  local copies, waits for them, and re-layouts: 32.9 us -> 16 us
    psum x2 -> x0, waiting for transfers between devices: 305 us -> none  [the longest x1 216 us: body(): dense = [t.astype(F32) for t in lax.psum(dense, ('dp', 'expert'))]]
    ppermute x0 -> x48, waiting for transfers between devices: none -> 133 us  [the longest x20 61 us: shift_inner(): return lax.ppermute(values, 'expert', pairs)]
    pallas_call x0 -> x14, Pallas kernels: none -> 96.1 us  [the longest x4 49.1 us: run_experts(): pl.pallas_call(functools.partial(expert_kernel, inner, len(buffers), expe...]
    ppermute x0 -> x48, starting transfers between devices: none -> 80.9 us  [the longest x15 41.9 us: shift_outer(): return lax.ppermute(values, 'expert', pairs)]
    dot_general x27 -> x8, matrix products: 89.9 us -> 20.7 us  [dot(): return jnp.einsum(spec, left, right, preferred_element_type=kind)]
    reduce_scatter x2 -> x1, waiting for transfers between devices: 64.8 us -> 0.01 us  [body(): lax.psum_scatter(after(mix_all, resid_full), 'expert', scatter_dimension=...]
    all_gather x2 -> x0, waiting for transfers between devices: 60.8 us -> none  [the longest x1 56.4 us: body(): lax.all_gather(normed_two.astype(BF16), 'expert', axis=0, tiled=True)]
    psum x1 -> x0, blocking collectives: 41 us -> none  [body(): lax.psum(jnp.stack([grad_attn_gain, grad_ffn_gain]), ('dp', 'expert', 'te...]
  transfers between devices with their start and end apart: 16 -> 60, of which waited for: 8 -> 25; matrix products, arithmetic and copies ran while one was open for 16% -> 16% of each run, Pallas kernels for 0% -> 23%
where the time goes in v2:
time: 419 us; the launch traced here: 411 us
  waiting for transfers between devices  135 us (32%)
  Pallas kernels  96.1 us (23%)
  starting transfers between devices  83.2 us (20%)
  other arithmetic  45.4 us (11%)
  matrix products  20.7 us (5%)
  local copies, waits for them, and re-layouts  16 us (4%)
  between operations  15 us (4%)
    ppermute x20, waiting for transfers between devices, shift_inner(): return lax.ppermute(values, 'expert', pairs)  61 us
    pallas_call x4, Pallas kernels, run_experts(): pl.pallas_call(functools.partial(expert_kernel, inner, len(buffers), expe...  49.1 us
    ppermute x15, starting transfers between devices, shift_outer(): return lax.ppermute(values, 'expert', pairs)  41.9 us
    ppermute x15, waiting for transfers between devices, shift_outer(): return lax.ppermute(values, 'expert', pairs)  33.8 us
    pallas_call x8, Pallas kernels, place_line(): pl.pallas_call(functools.partial(place_kernel, sizes, len(buffers)), out_...  23.4 us
    ppermute x5, waiting for transfers between devices, shift_dp(): lax.ppermute(values, 'dp', [(i, (i + step) % count) for i in range(count)])  22.7 us
    ppermute x20, starting transfers between devices, shift_inner(): return lax.ppermute(values, 'expert', pairs)  21.9 us
    dot_general x8, matrix products, dot(): return jnp.einsum(spec, left, right, preferred_element_type=kind)  20.7 us
  transfers between devices with their start and end apart: 60, of which 25 were waited for; matrix products, arithmetic and copies ran while one was open for 16% of the time, Pallas kernels for 23%

profile of v2, /device:TPU:0, one launch (start us, length us, event | category | flops | bytes accessed | tf_op | source)
XLA Modules:
  0.0 411.1 jit_solution(5484756710152603543)
XLA Ops:
  18.5 10.2 %shard_map.257 = (bf16[256,1536]{1,0:T(8,128)(2,1)}, bf16[256,768]{1,0:T(8,128)(2,1)}, bf16[256,256]{1,0:T(8,128)(2,1)}, bf16[256,256]{1,0:T(8,128)(2,1)}, bf16[...) custom-call(s32[2]{0:T(128)} %pad_add_fusion.meta, ...), custom_call_target="tpu_custom_call" | custom-call | flops 1 | bytes 1 | tf_op jit(solution)/shard_map/pallas_call | solution.py:192
  34.8 7.3 %collective-permute-done.6.refs_3_ = bf16[128,1664]{1,0:T(8,128)(2,1)S(1)} collective-permute-done((bf16[128,1664]{1,0:T(8,128)(2,1)S(1)}, bf16[128,1664]{1,0:T(8,128)(2,1)S(1)}, u32[]{:S(2)}, u32[]{:S(2)}) %collective-permute-start.6) | collective-permute-done | bytes 426016 | tf_op jit(solution)/shard_map/ppermute | solution.py:49
  46.1 6.7 %collective-permute-done.4.refs_1_ = bf16[128,1536]{1,0:T(8,128)(2,1)S(1)} collective-permute-done((bf16[128,1536]{1,0:T(8,128)(2,1)S(1)}, bf16[128,1536]{1,0:T(8,128)(2,1)S(1)}, u32[]{:S(2)}, u32[]{:S(2)}) %collective-permute-start.4) | collective-permute-done | bytes 393248 | tf_op jit(solution)/shard_map/ppermute | solution.py:49
  55.1 4.0 collective-permute-start.14
  63.6 12.2 %shard_map.258 = (bf16[1024,1536]{1,0:T(8,128)(2,1)}, bf16[1024,1536]{1,0:T(8,128)(2,1)}, bf16[1024,1536]{1,0:T(8,128)(2,1)}, bf16[2,1024,256]{2,1,0:T(8,128)(2,...) custom-call(s32[3]{0:T(128)} %get-tuple-element.488.meta, ...), custom_call_target="tpu_custom_call" | custom-call | flops 1 | bytes 1 | tf_op jit(solution)/shard_map/pallas_call | solution.py:347
  77.9 14.7 %collective-permute-start.16 = (bf16[128,1536]{1,0:T(8,128)(2,1)}, bf16[128,1536]{1,0:T(8,128)(2,1)S(1)}, u32[]{:S(2)}, u32[]{:S(2)}) collective-permute-start(bf16[128,1536]{1,0:T(8,128)(2,1)} %collective-permute-done.12.refs_0_), channel_id=1, source_target_pairs={{4,0},{6,2},{8,4},{10,6},{12,8},{14,10},{0,12},{2,14},{5,1},{7,3},... | collective-permute-start | bytes 1179656 | tf_op jit(solution)/shard_map/ppermute | solution.py:43
  93.2 12.3 %shard_map.259 = (bf16[1024,1536]{1,0:T(8,128)(2,1)}, bf16[1024,1536]{1,0:T(8,128)(2,1)}, bf16[1024,1536]{1,0:T(8,128)(2,1)}, bf16[2,1024,256]{2,1,0:T(8,128)(2,...) custom-call(s32[3]{0:T(128)} %get-tuple-element.489.meta, ...), custom_call_target="tpu_custom_call", output_to_operand_aliasing={{0}: (11, {}), {1}: (12, {}), {2}: (13, {}), {3}: (14, {}),... | custom-call | flops 1 | bytes 1 | tf_op jit(solution)/shard_map/pallas_call | solution.py:347
  109.2 12.3 %shard_map.260 = (bf16[1024,1536]{1,0:T(8,128)(2,1)}, bf16[1024,1536]{1,0:T(8,128)(2,1)}, bf16[1024,1536]{1,0:T(8,128)(2,1)}, bf16[2,1024,256]{2,1,0:T(8,128)(2,...) custom-call(s32[3]{0:T(128)} %get-tuple-element.490.meta, ...), custom_call_target="tpu_custom_call", output_to_operand_aliasing={{0}: (11, {}), {1}: (12, {}), {2}: (13, {}), {3}: (14, {}),... | custom-call | flops 1 | bytes 1 | tf_op jit(solution)/shard_map/pallas_call | solution.py:347
  121.7 10.1 %collective-permute-done.18.refs_1_ = bf16[128,1536]{1,0:T(8,128)(2,1)S(1)} collective-permute-done((bf16[128,1536]{1,0:T(8,128)(2,1)S(1)}, bf16[128,1536]{1,0:T(8,128)(2,1)S(1)}, u32[]{:S(2)}, u32[]{:S(2)}) %collective-permute-start.18) | collective-permute-done | bytes 393248 | tf_op jit(solution)/shard_map/ppermute | solution.py:49
  134.4 12.3 %shard_map.261 = (bf16[1024,1536]{1,0:T(8,128)(2,1)}, bf16[1024,1536]{1,0:T(8,128)(2,1)}, bf16[1024,1536]{1,0:T(8,128)(2,1)}, bf16[2,1024,256]{2,1,0:T(8,128)(2,...) custom-call(s32[3]{0:T(128)} %get-tuple-element.487.meta, ...), custom_call_target="tpu_custom_call", output_to_operand_aliasing={{0}: (11, {}), {1}: (12, {}), {2}: (13, {}), {3}: (14, {}),... | custom-call | flops 1 | bytes 1 | tf_op jit(solution)/shard_map/pallas_call | solution.py:347
  160.2 9.6 %collective-permute-done.33 = bf16[128,1536]{1,0:T(8,128)(2,1)} collective-permute-done((bf16[128,1536]{1,0:T(8,128)(2,1)S(1)}, bf16[128,1536]{1,0:T(8,128)(2,1)}, u32[]{:S(2)}, u32[]{:S(2)}) %collective-permute-start.33) | collective-permute-done | bytes 393248 | tf_op jit(solution)/shard_map/ppermute | solution.py:31
  190.6 13.3 %shard_map.262 = (bf16[256,640]{1,0:T(8,128)(2,1)}, bf16[256,640]{1,0:T(8,128)(2,1)}, f32[128,1536]{1,0:T(8,128)}, f32[128,1536]{1,0:T(8,128)}) custom-call(s32[2]{0:T(128)} %pad_add_fusion.meta, bf16[256,1536]{1,0:T(8,128)(2,1)} %copy-done.18, s32[1,256]{1,0:T(1,128)} %segs.3, f32[256,128]{1,0:T(8,128)} %constant.324.clone.cos_ref, ...), custom_call_target="tpu_custom_call" | custom-call | flops 1 | bytes 1 | tf_op jit(solution)/shard_map/pallas_call | solution.py:265
  209.4 4.5 %collective-permute-done.31 = bf16[256,640]{1,0:T(8,128)(2,1)} collective-permute-done((bf16[256,640]{1,0:T(8,128)(2,1)}, bf16[256,640]{1,0:T(8,128)(2,1)}, u32[]{:S(2)}, u32[]{:S(2)}) %collective-permute-start.31) | collective-permute-done | bytes 327712 | tf_op jit(solution)/shard_map/ppermute | solution.py:31
  219.7 8.2 %collective-permute-done.36 = bf16[192,1024]{1,0:T(8,128)(2,1)} collective-permute-done((bf16[192,1024]{1,0:T(8,128)(2,1)}, bf16[192,1024]{1,0:T(8,128)(2,1)}, u32[]{:S(2)}, u32[]{:S(2)}) %collective-permute-start.36) | collective-permute-done | bytes 393248 | tf_op jit(solution)/shard_map/ppermute | solution.py:49
  240.9 4.0 collective-permute-done.38
  247.5 4.3 %collective-permute-start.40 = (bf16[192,1024]{1,0:T(8,128)(2,1)}, bf16[192,1024]{1,0:T(8,128)(2,1)}, u32[]{:S(2)}, u32[]{:S(2)}) collective-permute-start(bf16[192,1024]{1,0:T(8,128)(2,1)} %add_convert_fusion.3), channel_id=1, source_target_pairs={{4,0},{6,2},{8,4},{10,6},{12,8},{14,10},{0,12},{2,14},{5,1},{7,3},... | collective-permute-start | bytes 1179656 | tf_op jit(solution)/shard_map/ppermute | solution.py:43
  255.7 13.0 %collective-permute-done.40 = bf16[192,1024]{1,0:T(8,128)(2,1)} collective-permute-done((bf16[192,1024]{1,0:T(8,128)(2,1)}, bf16[192,1024]{1,0:T(8,128)(2,1)}, u32[]{:S(2)}, u32[]{:S(2)}) %collective-permute-start.40) | collective-permute-done | bytes 393248 | tf_op jit(solution)/shard_map/ppermute | solution.py:43
  276.4 4.8 %collective-permute-done.41 = bf16[192,1024]{1,0:T(8,128)(2,1)} collective-permute-done((bf16[192,1024]{1,0:T(8,128)(2,1)}, bf16[192,1024]{1,0:T(8,128)(2,1)}, u32[]{:S(2)}, u32[]{:S(2)}) %collective-permute-start.41) | collective-permute-done | bytes 393248 | tf_op jit(solution)/shard_map/ppermute | solution.py:49
  287.4 8.3 %collective-permute-done.49 = bf16[192,1024]{1,0:T(8,128)(2,1)S(1)} collective-permute-done((bf16[192,1024]{1,0:T(8,128)(2,1)S(1)}, bf16[192,1024]{1,0:T(8,128)(2,1)S(1)}, u32[]{:S(2)}, u32[]{:S(2)}) %collective-permute-start.49) | collective-permute-done | bytes 393248 | tf_op jit(solution)/shard_map/ppermute | solution.py:31
  301.2 17.8 %collective-permute-done.50.block_ref = bf16[2,192,1024]{2,1,0:T(8,128)(2,1)S(1)} collective-permute-done((bf16[2,192,1024]{2,1,0:T(8,128)(2,1)S(1)}, bf16[2,192,1024]{2,1,0:T(8,128)(2,1)S(1)}, u32[]{:S(2)}, u32[]{:S(2)}) %collective-permute-start.50) | collective-permute-done | bytes 786464 | tf_op jit(solution)/shard_map/ppermute | solution.py:49
  319.0 9.9 %collective-permute-done.51.block_ref = bf16[2,192,1024]{2,1,0:T(8,128)(2,1)S(1)} collective-permute-done((bf16[2,192,1024]{2,1,0:T(8,128)(2,1)S(1)}, bf16[2,192,1024]{2,1,0:T(8,128)(2,1)S(1)}, u32[]{:S(2)}, u32[]{:S(2)}) %collective-permute-start.51) | collective-permute-done | bytes 786464 | tf_op jit(solution)/shard_map/ppermute | solution.py:43
  331.0 10.0 %collective-permute-done.45 = f32[2,1536]{1,0:T(2,128)S(1)} collective-permute-done((f32[2,1536]{1,0:T(2,128)S(1)}, f32[2,1536]{1,0:T(2,128)S(1)}, u32[]{:S(2)}, u32[]{:S(2)}) %collective-permute-start.45) | collective-permute-done | bytes 12320 | tf_op jit(solution)/shard_map/ppermute | solution.py:74
  382.9 3.9 convert_add_fusion.1
  395.1 5.4 %collective-permute-done.58 = bf16[2,256,1536]{2,1,0:T(8,128)(2,1)} collective-permute-done((bf16[2,256,1536]{2,1,0:T(8,128)(2,1)S(1)}, bf16[2,256,1536]{2,1,0:T(8,128)(2,1)}, u32[]{:S(2)}, u32[]{:S(2)}) %collective-permute-start.58) | collective-permute-done | bytes 1572896 | tf_op jit(solution)/shard_map/ppermute | solution.py:507
  (300 shorter events, 176.7 us)
Async XLA Ops:
  7.2 385.5 %reduce-scatter.2.cloned.1.call-start = ((), (), s32[]{:S(2)}) async-start(), calls=%async_computation.1 | async-start | bytes 3538944 | tf_op jit(solution)/shard_map/reduce_scatter | solution.py:525
  9.1 19.6 %collective-permute-start.1 = (bf16[128,1664]{1,0:T(8,128)(2,1)S(1)}, bf16[128,1664]{1,0:T(8,128)(2,1)}, u32[]{:S(2)}, u32[]{:S(2)}) collective-permute-start(bf16[128,1664]{1,0:T(8,128)(2,1)S(1)} %fusion.47.refs_2_), channel_id=1, source_target_pairs={{2,0},{0,2},{6,4},{4,6},{10,8},{8,10},{14,12},{12,14},{3,1},{1,3},... | collective-permute-start | bytes 1277960 | tf_op jit(solution)/shard_map/ppermute | solution.py:49
  29.3 29.8 %collective-permute-start.10 = (bf16[2,1536,256]{2,1,0:T(8,128)(2,1)S(1)}, bf16[2,1536,256]{2,1,0:T(8,128)(2,1)S(1)}, u32[]{:S(2)}, u32[]{:S(2)}) collective-permute-start(bf16[2,1536,256]{2,1,0:T(8,128)(2,1)S(1)} %copy-done.3), channel_id=1, source_target_pairs={{0,1},{1,0},{2,3},{3,2},{4,5},{5,4},{6,7},{7,6},{8,9},{9,8},{10,11... | collective-permute-start | bytes 4718600 | tf_op jit(solution)/shard_map/ppermute | solution.py:26
  29.4 29.8 %collective-permute-start.11 = (bf16[2,256,1536]{2,1,0:T(8,128)(2,1)S(1)}, bf16[2,256,1536]{2,1,0:T(8,128)(2,1)S(1)}, u32[]{:S(2)}, u32[]{:S(2)}) collective-permute-start(bf16[2,256,1536]{2,1,0:T(8,128)(2,1)S(1)} %copy-done.4), channel_id=1, source_target_pairs={{0,1},{1,0},{2,3},{3,2},{4,5},{5,4},{6,7},{7,6},{8,9},{9,8},{10,11... | collective-permute-start | bytes 4718600 | tf_op jit(solution)/shard_map/ppermute | solution.py:26
  29.8 33.7 %collective-permute-start.9 = (bf16[2,1536,256]{2,1,0:T(8,128)(2,1)S(1)}, bf16[2,1536,256]{2,1,0:T(8,128)(2,1)}, u32[]{:S(2)}, u32[]{:S(2)}) collective-permute-start(bf16[2,1536,256]{2,1,0:T(8,128)(2,1)S(1)} %copy-done.2), channel_id=1, source_target_pairs={{0,1},{1,0},{2,3},{3,2},{4,5},{5,4},{6,7},{7,6},{8,9},{9,8},{10,11... | collective-permute-start | bytes 4718600 | tf_op jit(solution)/shard_map/ppermute | solution.py:26
  54.5 21.2 %collective-permute-start.13 = (bf16[128,1664]{1,0:T(8,128)(2,1)}, bf16[128,1664]{1,0:T(8,128)(2,1)S(1)}, u32[]{:S(2)}, u32[]{:S(2)}) collective-permute-start(bf16[128,1664]{1,0:T(8,128)(2,1)} %collective-permute-done.7.refs_2_), channel_id=1, source_target_pairs={{2,0},{0,2},{6,4},{4,6},{10,8},{8,10},{14,12},{12,14},{3,1},{1,3},... | collective-permute-start | bytes 1277960 | tf_op jit(solution)/shard_map/ppermute | solution.py:49
  55.1 20.7 %collective-permute-start.14 = (bf16[128,1664]{1,0:T(8,128)(2,1)}, bf16[128,1664]{1,0:T(8,128)(2,1)S(1)}, u32[]{:S(2)}, u32[]{:S(2)}) collective-permute-start(bf16[128,1664]{1,0:T(8,128)(2,1)} %collective-permute-done.7.refs_2_), channel_id=1, source_target_pairs={{4,0},{6,2},{8,4},{10,6},{12,8},{14,10},{0,12},{2,14},{5,1},{7,3},... | collective-permute-start | bytes 1277960 | tf_op jit(solution)/shard_map/ppermute | solution.py:43
  75.8 29.8 %collective-permute-start.17 = (bf16[128,1664]{1,0:T(8,128)(2,1)S(1)}, bf16[128,1664]{1,0:T(8,128)(2,1)S(1)}, u32[]{:S(2)}, u32[]{:S(2)}) collective-permute-start(bf16[128,1664]{1,0:T(8,128)(2,1)S(1)} %collective-permute-done.14.refs_2_), channel_id=1, source_target_pairs={{2,0},{0,2},{6,4},{4,6},{10,8},{8,10},{14,12},{12,14},{3,1},{1,3},... | collective-permute-start | bytes 1277960 | tf_op jit(solution)/shard_map/ppermute | solution.py:49
  77.1 28.5 %collective-permute-start.15 = (bf16[128,1536]{1,0:T(8,128)(2,1)}, bf16[128,1536]{1,0:T(8,128)(2,1)S(1)}, u32[]{:S(2)}, u32[]{:S(2)}) collective-permute-start(bf16[128,1536]{1,0:T(8,128)(2,1)} %collective-permute-done.12.refs_0_), channel_id=1, source_target_pairs={{2,0},{0,2},{6,4},{4,6},{10,8},{8,10},{14,12},{12,14},{3,1},{1,3},... | collective-permute-start | bytes 1179656 | tf_op jit(solution)/shard_map/ppermute | solution.py:49
  77.9 27.7 %collective-permute-start.16 = (bf16[128,1536]{1,0:T(8,128)(2,1)}, bf16[128,1536]{1,0:T(8,128)(2,1)S(1)}, u32[]{:S(2)}, u32[]{:S(2)}) collective-permute-start(bf16[128,1536]{1,0:T(8,128)(2,1)} %collective-permute-done.12.refs_0_), channel_id=1, source_target_pairs={{4,0},{6,2},{8,4},{10,6},{12,8},{14,10},{0,12},{2,14},{5,1},{7,3},... | collective-permute-start | bytes 1179656 | tf_op jit(solution)/shard_map/ppermute | solution.py:43
  107.2 26.1 %collective-permute-start.21 = (bf16[128,1536]{1,0:T(8,128)(2,1)S(1)}, bf16[128,1536]{1,0:T(8,128)(2,1)S(1)}, u32[]{:S(2)}, u32[]{:S(2)}) collective-permute-start(bf16[128,1536]{1,0:T(8,128)(2,1)S(1)} %copy-done.55), channel_id=1, source_target_pairs={{2,0},{0,2},{6,4},{4,6},{10,8},{8,10},{14,12},{12,14},{3,1},{1,3},... | collective-permute-start | bytes 1179656 | tf_op jit(solution)/shard_map/ppermute | solution.py:49
  107.7 24.1 %collective-permute-start.18 = (bf16[128,1536]{1,0:T(8,128)(2,1)S(1)}, bf16[128,1536]{1,0:T(8,128)(2,1)S(1)}, u32[]{:S(2)}, u32[]{:S(2)}) collective-permute-start(bf16[128,1536]{1,0:T(8,128)(2,1)S(1)} %collective-permute-done.16.refs_0_), channel_id=1, source_target_pairs={{2,0},{0,2},{6,4},{4,6},{10,8},{8,10},{14,12},{12,14},{3,1},{1,3},... | collective-permute-start | bytes 1179656 | tf_op jit(solution)/shard_map/ppermute | solution.py:49
  158.2 17.6 %collective-permute-start.26 = (bf16[2,1536,256]{2,1,0:T(8,128)(2,1)S(1)}, bf16[2,1536,256]{2,1,0:T(8,128)(2,1)S(1)}, u32[]{:S(2)}, u32[]{:S(2)}) collective-permute-start(bf16[2,1536,256]{2,1,0:T(8,128)(2,1)S(1)} %fusion.23), channel_id=1, source_target_pairs={{0,1},{1,0},{2,3},{3,2},{4,5},{5,4},{6,7},{7,6},{8,9},{9,8},{10,11... | collective-permute-start | bytes 4718600 | tf_op jit(solution)/shard_map/ppermute | solution.py:26
  184.0 22.0 %collective-permute-start.35 = (bf16[256,768]{1,0:T(8,128)(2,1)}, bf16[256,768]{1,0:T(8,128)(2,1)S(1)}, u32[]{:S(2)}, u32[]{:S(2)}) collective-permute-start(bf16[256,768]{1,0:T(8,128)(2,1)} %get-tuple-element.371.mixed_ref), channel_id=1, source_target_pairs={{0,16},{16,0},{1,17},{17,1},{2,18},{18,2},{3,19},{19,3},{4,20},{20... | collective-permute-start | bytes 1179656 | tf_op jit(solution)/shard_map/ppermute | solution.py:31
  187.5 16.7 %collective-permute-start.30 = (bf16[256,768]{1,0:T(8,128)(2,1)S(1)}, bf16[256,768]{1,0:T(8,128)(2,1)S(1)}, u32[]{:S(2)}, u32[]{:S(2)}) collective-permute-start(bf16[256,768]{1,0:T(8,128)(2,1)S(1)} %get-tuple-element.477), channel_id=1, source_target_pairs={{0,16},{16,0},{1,17},{17,1},{2,18},{18,2},{3,19},{19,3},{4,20},{20... | collective-permute-start | bytes 1179656 | tf_op jit(solution)/shard_map/ppermute | solution.py:31
  235.1 49.7 %collective-permute-start.32 = (bf16[2,1536,256]{2,1,0:T(8,128)(2,1)}, bf16[2,1536,256]{2,1,0:T(8,128)(2,1)}, u32[]{:S(2)}, u32[]{:S(2)}) collective-permute-start(bf16[2,1536,256]{2,1,0:T(8,128)(2,1)} %fusion.17), channel_id=1, source_target_pairs={{0,16},{16,0},{1,17},{17,1},{2,18},{18,2},{3,19},{19,3},{4,20},{20... | collective-permute-start | bytes 4718600 | tf_op jit(solution)/shard_map/ppermute | solution.py:507
  247.5 21.2 %collective-permute-start.40 = (bf16[192,1024]{1,0:T(8,128)(2,1)}, bf16[192,1024]{1,0:T(8,128)(2,1)}, u32[]{:S(2)}, u32[]{:S(2)}) collective-permute-start(bf16[192,1024]{1,0:T(8,128)(2,1)} %add_convert_fusion.3), channel_id=1, source_target_pairs={{4,0},{6,2},{8,4},{10,6},{12,8},{14,10},{0,12},{2,14},{5,1},{7,3},... | collective-permute-start | bytes 1179656 | tf_op jit(solution)/shard_map/ppermute | solution.py:43
  295.8 23.2 %collective-permute-start.50 = (bf16[2,192,1024]{2,1,0:T(8,128)(2,1)S(1)}, bf16[2,192,1024]{2,1,0:T(8,128)(2,1)S(1)}, u32[]{:S(2)}, u32[]{:S(2)}) collective-permute-start(bf16[2,192,1024]{2,1,0:T(8,128)(2,1)S(1)} %pad_maximum_fusion.2.block_ref), channel_id=1, source_target_pairs={{2,0},{0,2},{6,4},{4,6},{10,8},{8,10},{14,12},{12,14},{3,1},{1,3},... | collective-permute-start | bytes 2359304 | tf_op jit(solution)/shard_map/ppermute | solution.py:49
  296.6 32.3 %collective-permute-start.51 = (bf16[2,192,1024]{2,1,0:T(8,128)(2,1)S(1)}, bf16[2,192,1024]{2,1,0:T(8,128)(2,1)S(1)}, u32[]{:S(2)}, u32[]{:S(2)}) collective-permute-start(bf16[2,192,1024]{2,1,0:T(8,128)(2,1)S(1)} %pad_maximum_fusion.2.block_ref), channel_id=1, source_target_pairs={{4,0},{6,2},{8,4},{10,6},{12,8},{14,10},{0,12},{2,14},{5,1},{7,3},... | collective-permute-start | bytes 2359304 | tf_op jit(solution)/shard_map/ppermute | solution.py:43
  299.4 29.6 %collective-permute-start.44 = (f32[2,1536]{1,0:T(2,128)S(1)}, f32[2,1536]{1,0:T(2,128)S(1)}, u32[]{:S(2)}, u32[]{:S(2)}) collective-permute-start(f32[2,1536]{1,0:T(2,128)S(1)} %pad_maximum_fusion.4), channel_id=1, source_target_pairs={{0,1},{1,0},{2,3},{3,2},{4,5},{5,4},{6,7},{7,6},{8,9},{9,8},{10,11... | collective-permute-start | bytes 36872 | tf_op jit(solution)/shard_map/ppermute | solution.py:74
  299.5 70.2 %collective-permute-start.56 = (bf16[2,1536,256]{2,1,0:T(8,128)(2,1)}, bf16[2,1536,256]{2,1,0:T(8,128)(2,1)}, u32[]{:S(2)}, u32[]{:S(2)}) collective-permute-start(bf16[2,1536,256]{2,1,0:T(8,128)(2,1)} %fusion.14), channel_id=1, source_target_pairs={{0,16},{16,0},{1,17},{17,1},{2,18},{18,2},{3,19},{19,3},{4,20},{20... | collective-permute-start | bytes 4718600 | tf_op jit(solution)/shard_map/ppermute | solution.py:507
  328.9 26.9 %collective-permute-start.52 = (bf16[2,192,1024]{2,1,0:T(8,128)(2,1)S(1)}, bf16[2,192,1024]{2,1,0:T(8,128)(2,1)}, u32[]{:S(2)}, u32[]{:S(2)}) collective-permute-start(bf16[2,192,1024]{2,1,0:T(8,128)(2,1)S(1)} %collective-permute-done.51.block_ref), channel_id=1, source_target_pairs={{2,0},{0,2},{6,4},{4,6},{10,8},{8,10},{14,12},{12,14},{3,1},{1,3},... | collective-permute-start | bytes 2359304 | tf_op jit(solution)/shard_map/ppermute | solution.py:49
  328.9 26.9 %collective-permute-start.53 = (bf16[2,192,1024]{2,1,0:T(8,128)(2,1)S(1)}, bf16[2,192,1024]{2,1,0:T(8,128)(2,1)}, u32[]{:S(2)}, u32[]{:S(2)}) collective-permute-start(bf16[2,192,1024]{2,1,0:T(8,128)(2,1)S(1)} %collective-permute-done.51.block_ref), channel_id=1, source_target_pairs={{4,0},{6,2},{8,4},{10,6},{12,8},{14,10},{0,12},{2,14},{5,1},{7,3},... | collective-permute-start | bytes 2359304 | tf_op jit(solution)/shard_map/ppermute | solution.py:43
  370.4 30.1 %collective-permute-start.58 = (bf16[2,256,1536]{2,1,0:T(8,128)(2,1)S(1)}, bf16[2,256,1536]{2,1,0:T(8,128)(2,1)}, u32[]{:S(2)}, u32[]{:S(2)}) collective-permute-start(bf16[2,256,1536]{2,1,0:T(8,128)(2,1)S(1)} %copy-done.19), channel_id=1, source_target_pairs={{0,16},{16,0},{1,17},{17,1},{2,18},{18,2},{3,19},{19,3},{4,20},{20... | collective-permute-start | bytes 4718600 | tf_op jit(solution)/shard_map/ppermute | solution.py:507
  (93 other events, 1032.6 us)
Sparse Core Ops, SparseCore 0:
  235.2 94.8 reduce-scatter.1
